TPU v7x, 32 devices: a whole 2x2x4 slice. The times are simulated.
32 devices in a mesh: seq: 8 (over y, x, core), tp: 4 (over z).
Axes of the slice: x: 2, y: 2, z: 4, core: 2. Of those that a mesh axis runs over, the one named last changes fastest.
Arguments:
- hidden: bfloat16 [10240, 8192], P('seq', 'tp'), may hold values from -6 to 6
- queries: bfloat16 [10240, 8192], P('seq', 'tp'), may hold values from -8 to 8
- keys_values: bfloat16 [2, 10240, 1024], P(None, 'seq', 'tp'), may hold values from -8 to 8
- w_router: bfloat16 [8192], P('tp'), may hold values from -0.0625 to 0.0625
- routed: int32 [8, 160], P('seq'), may hold values from 0 to 1279, as said below
- counts: int32 [8], replicated, may hold values from 1 to 160, 800 in all
- grad_out: bfloat16 [1280, 8192], P('seq', 'tp'), may hold values from -6 to 6
Outputs:
- branch_out: bfloat16 [1280, 8192], P('seq', 'tp')
- grad_queries: bfloat16 [1280, 8192], P('seq', 'tp')
- grad_keys_values: bfloat16 [2, 1280, 1024], P(None, 'seq', 'tp')
- grad_router: float32 [8192], P('tp')
Inputs may be any that keep to these rules, and one draw needn't show every extreme that they name: Each row lists 160 different positions of one shard's tokens in increasing order; the first counts entries of a row are the shard's routed tokens. `counts`: each shard has at least one live slot and one shard has all 160.
All inputs are finite; a program needn't handle non-finite values.
Results may differ from a plain program's by a relative error of at most 0.03.
Values may be sent and summed in bfloat16 or wider, within the bound.
No kernel may reach another device: no remote copies, remote signals or barrier semaphores. Data moves between devices by JAX's collectives and lax.ppermute only.
A program may use at most 128 MiB of HBM per device.

v0:
```python
import functools
import math

import jax
import jax.numpy as jnp
from jax import lax
from jax.experimental import pallas as pl
from jax.experimental.pallas import tpu as pltpu
from jax.sharding import PartitionSpec as P


HEAD_WIDTH = 128
LANES = 128
LOG2E = math.log2(math.e)
FAR = 1 << 30
BF16 = jnp.bfloat16
F32 = jnp.float32


def dot(a, b):
    return lax.dot_general(a, b, (((1,), (0,)), ((), ())), preferred_element_type=F32)


def eye(shape):
    return lax.broadcasted_iota(jnp.int32, shape, 0) == lax.broadcasted_iota(jnp.int32, shape, 1)


def row_to_column(row, rows):
    spread = jnp.broadcast_to(row, (rows, row.shape[1]))
    return jnp.sum(jnp.where(eye(spread.shape), spread, 0.0), axis=1, keepdims=True)


def column_to_row(column, width):
    spread = jnp.broadcast_to(column, (column.shape[0], width))
    return jnp.sum(jnp.where(eye(spread.shape), spread, 0.0), axis=0, keepdims=True)


def one_hot(routed_row, tokens):
    slots = routed_row.shape[1]
    column = row_to_column(routed_row.astype(F32), slots).astype(jnp.int32)
    ids = lax.broadcasted_iota(jnp.int32, (slots, tokens), 1)
    return jnp.where(ids == column, 1.0, 0.0).astype(BF16)


def rows_of(split, core, rows):
    if split == 1:
        return [rows]
    low, high = rows[:, :HEAD_WIDTH], rows[:, HEAD_WIDTH:]
    first = core == 0
    return [jnp.where(first, low, high), jnp.where(first, high, low)]


def pieces(rows, number=5):
    size = -(-rows // number // 16) * 16
    return [(at, min(size, rows - at)) for at in range(0, rows, size)]


def gather_first(keys_values, hidden, w_router, routed, core, split, wide):
    _, tokens, width = keys_values.shape
    model = hidden.shape[1]
    slots = routed.shape[1]
    step = 256
    parts = pieces(tokens)

    def body(core_ref, routed_ref, w_ref, kv_hbm, x_hbm, *refs):
        outs, (x_out, logit_ref, kv_buf, x_buf, acc, kv_sem, x_sem) = refs[:split], refs[split:]
        kv_copies = [
            pltpu.make_async_copy(kv_hbm.at[i], kv_buf.at[i], kv_sem.at[i]) for i in range(2)
        ]
        x_copies = [
            pltpu.make_async_copy(
                x_hbm.at[pl.ds(at, size)], x_buf.at[pl.ds(at, size)], x_sem.at[p]
            )
            for p, (at, size) in enumerate(parts)
        ]
        for copy in kv_copies + x_copies:
            copy.start()
        select = one_hot(routed_ref[...], tokens)
        for i in range(2):
            kv_copies[i].wait()
            rows = dot(select, kv_buf[i]).astype(BF16)
            for out, part in zip(outs, rows_of(split, core_ref[0], rows)):
                out[i] = part
        for copy in x_copies:
            copy.wait()
        acc[...] = jnp.zeros_like(acc)
        for j in range(model // step):
            rows = dot(select, x_buf[:, j * step : (j + 1) * step])
            x_out[:, j * step : (j + 1) * step] = rows.astype(BF16)
            for t in range(step // LANES):
                b = j * (step // LANES) + t
                weight = w_ref[b : b + 1, :].astype(F32)
                acc[...] += rows[:, t * LANES : (t + 1) * LANES] * weight
        logit_ref[...] = column_to_row(jnp.sum(acc[...], axis=1, keepdims=True), wide)

    return pl.pallas_call(
        body,
        grid_spec=pltpu.PrefetchScalarGridSpec(
            num_scalar_prefetch=1,
            grid=(1,),
            in_specs=[
                whole((1, slots)),
                whole((model // LANES, LANES)),
                pl.BlockSpec(memory_space=pltpu.HBM),
                pl.BlockSpec(memory_space=pltpu.HBM),
            ],
            out_specs=[whole((2, slots, HEAD_WIDTH))] * split
            + [whole((slots, model)), whole((1, wide))],
            scratch_shapes=[
                pltpu.VMEM((2, tokens, width), BF16),
                pltpu.VMEM((tokens, model), BF16),
                pltpu.VMEM((slots, LANES), F32),
                pltpu.SemaphoreType.DMA((2,)),
                pltpu.SemaphoreType.DMA((len(parts),)),
            ],
        ),
        out_shape=[jax.ShapeDtypeStruct((2, slots, HEAD_WIDTH), BF16)] * split
        + [
            jax.ShapeDtypeStruct((slots, model), BF16),
            jax.ShapeDtypeStruct((1, wide), F32),
        ],
        compiler_params=pltpu.CompilerParams(vmem_limit_bytes=58 << 20),
        name="gather_first",
    )(core, routed, w_router.reshape(model // LANES, LANES), keys_values, hidden)


def gather_queries(queries, routed, grad_out, core, split, after):
    tokens, width = queries.shape
    slots = routed.shape[1]
    half = width // split
    step = 256
    parts = pieces(tokens)

    def body(core_ref, routed_ref, g_hbm, q_hbm, *refs):
        refs = refs[len(after) :]
        outs, (g_buf, q_buf, rows_buf, sem, g_sem, out_sem) = refs[:split], refs[split:]
        copies = [
            pltpu.make_async_copy(q_hbm.at[pl.ds(at, size)], q_buf.at[pl.ds(at, size)], sem.at[p])
            for p, (at, size) in enumerate(parts)
        ]
        load = pltpu.make_async_copy(g_hbm, g_buf, g_sem)
        for copy in copies + [load]:
            copy.start()
        select = one_hot(routed_ref[...], tokens)

        def give(source, kind):
            for h in range(split):
                columns = pl.ds(h * half, half)
                for o in range(split):
                    copy = pltpu.make_async_copy(
                        source.at[:, columns], outs[o].at[kind], out_sem.at[kind, h]
                    )
                    if split == 1:
                        copy.start()
                    else:
                        pl.when(core_ref[0] == (h ^ o))(copy.start)

        load.wait()
        give(g_buf, 1)
        for copy in copies:
            copy.wait()
        for j in range(width // step):
            at = slice(j * step, (j + 1) * step)
            rows_buf[:, at] = dot(select, q_buf[:, at]).astype(BF16)
        give(rows_buf, 0)
        for kind in range(2):
            for h in range(split):
                pltpu.make_async_copy(
                    g_buf.at[:, pl.ds(h * half, half)], outs[0].at[kind], out_sem.at[kind, h]
                ).wait()

    return pl.pallas_call(
        body,
        grid_spec=pltpu.PrefetchScalarGridSpec(
            num_scalar_prefetch=1,
            grid=(1,),
            in_specs=[whole((1, slots))]
            + [pl.BlockSpec(memory_space=pltpu.HBM)] * 2
            + [pl.BlockSpec(memory_space=pl.ANY)] * len(after),
            out_specs=[pl.BlockSpec(memory_space=pl.ANY)] * split,
            scratch_shapes=[
                pltpu.VMEM((slots, width), BF16),
                pltpu.VMEM((tokens, width), BF16),
                pltpu.VMEM((slots, width), BF16),
                pltpu.SemaphoreType.DMA((len(parts),)),
                pltpu.SemaphoreType.DMA,
                pltpu.SemaphoreType.DMA((2, split)),
            ],
        ),
        out_shape=[jax.ShapeDtypeStruct((2, slots, half), BF16)] * split,
        compiler_params=pltpu.CompilerParams(vmem_limit_bytes=16 << 20),
        name="gather_queries",
    )(core, routed, grad_out, queries, *after)


class Plan:
    def __init__(self, seq, split, slots, group, wide):
        self.seq, self.split, self.slots, self.group, self.wide = seq, split, slots, group, wide
        self.tile = 256
        self.tiles = -(-seq * slots // self.tile)
        self.keys = self.tiles * self.tile
        self.rows = 32
        self.chunks = slots // self.rows
        self.lanes = self.rows * group
        self.blocks = seq // split


def stack_heads(block, plan):
    return jnp.concatenate(
        [block[:, h * HEAD_WIDTH : (h + 1) * HEAD_WIDTH] for h in range(plan.group)], axis=0
    )


def whole(shape):
    return pl.BlockSpec(shape, lambda *_: (0,) * len(shape))


def total_of(refs, side):
    total = refs[0][side : side + 1, :]
    for ref in refs[1:]:
        total = total + ref[side : side + 1, :]
    return total


def gate_of(logit):
    return 1.0 / (1.0 + jnp.exp(-logit))


def repeat(tiles, step, carried):
    if isinstance(tiles, int):
        for t in range(tiles):
            carried = step(t, carried)
        return carried
    return lax.fori_loop(0, tiles, step, carried)


def attend(plan, shard, counts, blocks, sides, logits):
    seq, split, slots, tile, lanes = plan.seq, plan.split, plan.slots, plan.tile, plan.lanes
    inverse = 1.0 / math.sqrt(HEAD_WIDTH)
    scale = LOG2E * inverse
    reps = lanes // LANES
    width = plan.group * HEAD_WIDTH

    def body(shard_ref, counts_ref, *refs):
        refs = list(refs)
        block_refs = [refs.pop(0) for _ in range(plan.blocks)]
        side_hbm = [refs.pop(0) for _ in range(split)]
        logit_refs = [refs.pop(0) for _ in range(len(logits))]
        out_hbm = [refs.pop(0) for _ in range(split)]
        back_refs = [refs.pop(0) for _ in range(plan.blocks)]
        gate_ref = refs.pop(0)
        (side_buf, out_buf, keys, values, place, keys_t, values_t, scores) = refs[:8]
        (key_acc, value_acc, columns, gate_column, starts, in_sem, out_sem) = refs[8:]
        fetch = [
            pltpu.make_async_copy(side_hbm[i], side_buf.at[i], in_sem.at[i]) for i in range(split)
        ]
        for copy in fetch:
            copy.start()
        own = shard_ref[0]
        end = jnp.int32(0)
        for j in range(seq):
            starts[j] = end
            end = end + ((counts_ref[j] + 15) // 16) * 16
        for b in range(plan.blocks):
            for i in range(split):
                source = own ^ (b * split + i)
                live = counts_ref[source]
                start = starts[source]

                def move(t, _, b=b, i=i, live=live, start=start):
                    at = pl.multiple_of(t * 16, 16)
                    to = pl.multiple_of(start + t * 16, 16)
                    keys[pl.ds(to, 16), :] = block_refs[b][i, 0, pl.ds(at, 16), :]
                    values[pl.ds(to, 16), :] = block_refs[b][i, 1, pl.ds(at, 16), :]
                    slot = at + lax.broadcasted_iota(jnp.int32, (16, LANES), 0)
                    place[pl.ds(to, 16), :] = jnp.where(slot < live, start + slot, FAR)
                    return 0

                lax.fori_loop(0, (live + 15) // 16, move, 0)
        tail = pl.ds(pl.multiple_of(end, 16), tile)
        keys[tail, :] = jnp.zeros((tile, HEAD_WIDTH), BF16)
        values[tail, :] = jnp.zeros((tile, HEAD_WIDTH), BF16)
        place[tail, :] = jnp.full((tile, LANES), FAR, jnp.int32)

        def prepare(t, _):
            here = pl.ds(pl.multiple_of(t * tile, tile), tile)
            keys_t[:, here] = keys[here, :].T
            values_t[:, here] = values[here, :].T
            key_acc[here, :] = jnp.zeros((tile, HEAD_WIDTH), F32)
            value_acc[here, :] = jnp.zeros((tile, HEAD_WIDTH), F32)
            return 0

        lax.fori_loop(0, (end + tile - 1) // tile, prepare, 0)
        gate_column[...] = jnp.zeros_like(gate_column)
        for side in range(split):
            weight = gate_of(total_of(logit_refs, side))
            slot = lax.broadcasted_iota(jnp.int32, weight.shape, 1)
            weight = jnp.where(slot < counts_ref[own ^ side], weight, 0.0)
            for b in range(plan.wide // LANES):
                at = slice(b * LANES, (b + 1) * LANES)
                column = row_to_column(weight[:, at], LANES)
                columns[side, at, :] = jnp.broadcast_to(column, (LANES, LANES))
        for copy in fetch:
            copy.wait()

        def chunk_step(u, _):
            side = u // plan.chunks
            mine = own ^ side
            live = counts_ref[mine]
            offset = starts[mine]
            first = pl.multiple_of((u % plan.chunks) * plan.rows, plan.rows)
            at = pl.ds(first, plan.rows)
            needed = (offset + jnp.minimum(live, first + plan.rows) + tile - 1) // tile
            needed = jnp.where(first < live, needed, 0)

            @pl.when(needed == 0)
            def _():
                out_buf[side, :, at, :] = jnp.zeros((2, plan.rows, width), BF16)

            def work(tiles):
                q = stack_heads(side_buf[side, 0, at, :], plan)
                upstream = stack_heads(side_buf[side, 1, at, :], plan).astype(F32)
                weight = jnp.concatenate([columns[side, at, :]] * plan.group, axis=0)
                narrow = (upstream * weight).astype(BF16)
                q_t = q.T
                narrow_t = narrow.T
                lane = lax.broadcasted_iota(jnp.int32, (1, lanes), 1)
                positions = offset + first + lane % plan.rows

                def here_of(t):
                    if isinstance(t, int):
                        return slice(t * tile, (t + 1) * tile)
                    return pl.ds(pl.multiple_of(t * tile, tile), tile)

                def score(t, running):
                    here = here_of(t)
                    s = dot(keys[here, :], q_t) * scale
                    allowed = jnp.concatenate([place[here, :]] * reps, axis=1) <= positions
                    s = jnp.where(allowed, s, -jnp.inf)
                    scores[here, :] = s
                    return jnp.maximum(running, jnp.max(s, axis=0, keepdims=True))

                top = repeat(tiles, score, jnp.full((1, lanes), -1e30, F32))

                def spread(t, carried):
                    summed, out_t = carried
                    here = here_of(t)
                    p = jnp.exp2(scores[here, :] - top)
                    scores[here, :] = p
                    summed = summed + jnp.sum(p, axis=0, keepdims=True)
                    return (summed, out_t + dot(values_t[:, here], p.astype(BF16)))

                summed, out_t = repeat(
                    tiles,
                    spread,
                    (jnp.zeros((1, lanes), F32), jnp.zeros((HEAD_WIDTH, lanes), F32)),
                )
                share = 1.0 / summed
                out_t = out_t * share
                delta = jnp.sum(narrow_t.astype(F32) * out_t, axis=0, keepdims=True)

                def back(t, grad_t):
                    here = here_of(t)
                    p = scores[here, :] * share
                    dp = dot(values[here, :], narrow_t)
                    value_acc[here, :] += dot(p.astype(BF16), narrow)
                    ds = (p * (dp - delta)).astype(BF16)
                    key_acc[here, :] += dot(ds, q)
                    return grad_t + dot(keys_t[:, here], ds)

                grad_t = repeat(tiles, back, jnp.zeros((HEAD_WIDTH, lanes), F32))
                out = out_t.T
                raw = upstream * out
                gate = raw[: plan.rows]
                for h in range(1, plan.group):
                    gate = gate + raw[h * plan.rows : (h + 1) * plan.rows]
                gate_column[side, at, :] = gate
                weighted = (out * weight).astype(BF16)
                grad = (grad_t * inverse).astype(BF16).T
                for h in range(plan.group):
                    heads = slice(h * HEAD_WIDTH, (h + 1) * HEAD_WIDTH)
                    rows = slice(h * plan.rows, (h + 1) * plan.rows)
                    out_buf[side, 0, at, heads] = weighted[rows]
                    out_buf[side, 1, at, heads] = grad[rows]

            if plan.tiles <= 5:
                for tiles in range(1, plan.tiles + 1):
                    pl.when(needed == tiles)(functools.partial(work, tiles))
            else:
                pl.when(needed > 0)(functools.partial(work, needed))
            return 0

        lax.fori_loop(0, split * plan.chunks, chunk_step, 0)
        push = [
            pltpu.make_async_copy(out_buf.at[i], out_hbm[i], out_sem.at[i]) for i in range(split)
        ]
        for copy in push:
            copy.start()
        for side in range(split):
            gate_ref[side : side + 1, :] = column_to_row(
                jnp.sum(gate_column[side], axis=1, keepdims=True), plan.wide
            )
        for b in range(plan.blocks):
            back_refs[b][...] = jnp.zeros_like(back_refs[b])
            for i in range(split):
                source = own ^ (b * split + i)
                live = counts_ref[source]
                start = starts[source]

                def give(t, _, b=b, i=i, start=start):
                    at = pl.ds(pl.multiple_of(t * 16, 16), 16)
                    here = pl.ds(pl.multiple_of(start + t * 16, 16), 16)
                    back_refs[b][i, 0, at, :] = (key_acc[here, :] * inverse).astype(BF16)
                    back_refs[b][i, 1, at, :] = value_acc[here, :].astype(BF16)
                    return 0

                lax.fori_loop(0, (live + 15) // 16, give, 0)
        for copy in push:
            copy.wait()

    block = (split, 2, slots, HEAD_WIDTH)
    side = (2, slots, width)
    return pl.pallas_call(
        body,
        grid_spec=pltpu.PrefetchScalarGridSpec(
            num_scalar_prefetch=2,
            grid=(1,),
            in_specs=[whole(block)] * plan.blocks
            + [pl.BlockSpec(memory_space=pl.ANY)] * split
            + [whole((split, plan.wide))] * len(logits),
            out_specs=[pl.BlockSpec(memory_space=pl.ANY)] * split
            + [whole(block)] * plan.blocks
            + [whole((split, plan.wide))],
            scratch_shapes=[
                pltpu.VMEM((split,) + side, BF16),
                pltpu.VMEM((split,) + side, BF16),
                pltpu.VMEM((plan.keys + tile, HEAD_WIDTH), BF16),
                pltpu.VMEM((plan.keys + tile, HEAD_WIDTH), BF16),
                pltpu.VMEM((plan.keys + tile, LANES), jnp.int32),
                pltpu.VMEM((HEAD_WIDTH, plan.keys), BF16),
                pltpu.VMEM((HEAD_WIDTH, plan.keys), BF16),
                pltpu.VMEM((plan.keys, lanes), F32),
                pltpu.VMEM((plan.keys, HEAD_WIDTH), F32),
                pltpu.VMEM((plan.keys, HEAD_WIDTH), F32),
                pltpu.VMEM((split, plan.wide, LANES), F32),
                pltpu.VMEM((split, slots, LANES), F32),
                pltpu.SMEM((seq,), jnp.int32),
                pltpu.SemaphoreType.DMA((split,)),
                pltpu.SemaphoreType.DMA((split,)),
            ],
        ),
        out_shape=[jax.ShapeDtypeStruct(side, BF16)] * split
        + [jax.ShapeDtypeStruct(block, BF16)] * plan.blocks
        + [jax.ShapeDtypeStruct((split, plan.wide), F32)],
        compiler_params=pltpu.CompilerParams(
            vmem_limit_bytes=(24 << 20) if plan.tiles <= 5 else (48 << 20)
        ),
        name="attend",
    )(shard, counts, *blocks, *sides, *logits)


def router_part(shard, counts, logits, gates, rows, wide, after):
    slots, width = rows[0].shape
    split = len(rows)
    number = len(logits)

    def body(shard_ref, counts_ref, *refs):
        logit_refs, gate_refs = refs[:number], refs[number : 2 * number]
        row_refs, out_ref = refs[2 * number : 2 * number + split], refs[-1]
        columns = []
        for side in range(split):
            gate = gate_of(total_of(logit_refs, side))
            term = total_of(gate_refs, side)
            slot = lax.broadcasted_iota(jnp.int32, gate.shape, 1)
            live = slot < counts_ref[shard_ref[0] ^ side]
            columns.append(
                jnp.broadcast_to(
                    row_to_column(jnp.where(live, term * gate * (1.0 - gate), 0.0), slots),
                    (slots, LANES),
                )
            )
        for b in range(width // LANES):
            at = slice(b * LANES, (b + 1) * LANES)
            product = row_refs[0][:, at].astype(F32) * columns[0]
            for side in range(1, split):
                product = product + row_refs[side][:, at].astype(F32) * columns[side]
            out_ref[b : b + 1, :] = jnp.sum(product, axis=0, keepdims=True)

    return pl.pallas_call(
        body,
        grid_spec=pltpu.PrefetchScalarGridSpec(
            num_scalar_prefetch=2,
            grid=(1,),
            in_specs=[whole((split, wide))] * (2 * number)
            + [whole((slots, width))] * split
            + [pl.BlockSpec(memory_space=pl.ANY)] * len(after),
            out_specs=whole((width // LANES, LANES)),
        ),
        out_shape=jax.ShapeDtypeStruct((width // LANES, LANES), F32),
        compiler_params=pltpu.CompilerParams(vmem_limit_bytes=16 << 20),
        name="router_part",
    )(shard, counts, *logits, *gates, *rows, *after)


def join_halves(core, mine, taken):
    _, slots, half = mine.shape

    def body(core_ref, mine_ref, taken_ref, *outs):
        for a in range(2):
            @pl.when(pl.program_id(0) == 0)
            def _(a=a):
                outs[a][...] = mine_ref[a]

            @pl.when(pl.program_id(0) == 1)
            def _(a=a):
                outs[a][...] = taken_ref[a]

    return pl.pallas_call(
        body,
        grid_spec=pltpu.PrefetchScalarGridSpec(
            num_scalar_prefetch=1,
            grid=(2,),
            in_specs=[whole((2, slots, half))] * 2,
            out_specs=[pl.BlockSpec((slots, half), lambda i, c: (0, i ^ c[0]))] * 2,
        ),
        out_shape=[jax.ShapeDtypeStruct((slots, 2 * half), BF16)] * 2,
        compiler_params=pltpu.CompilerParams(vmem_limit_bytes=16 << 20),
        name="join_halves",
    )(core, mine, taken)


def add_up(blocks, after):
    split = blocks[0].shape[0]
    number = len(blocks)
    shape = blocks[0].shape[1:]

    def body(*refs):
        ins, outs = refs[:number], refs[number + len(after) :]
        for side in range(split):
            acc = ins[0][side].astype(F32)
            for ref in ins[1:]:
                acc = acc + ref[side].astype(F32)
            outs[side][...] = acc.astype(BF16)

    return pl.pallas_call(
        body,
        grid=(1,),
        in_specs=[whole(blocks[0].shape)] * number
        + [pl.BlockSpec(memory_space=pl.ANY)] * len(after),
        out_specs=[whole(shape)] * split,
        out_shape=[jax.ShapeDtypeStruct(shape, BF16)] * split,
        compiler_params=pltpu.CompilerParams(vmem_limit_bytes=16 << 20),
        name="add_up",
    )(*blocks, *after)


def finish(core, mine, taken, routers):
    _, slots, head = mine.shape
    number = len(routers)

    def body(core_ref, mine_ref, taken_ref, *refs):
        out_ref, router_out = refs[number:]
        first = core_ref[0] == 0
        a, b = mine_ref[...], taken_ref[...]
        out_ref[:, :, :head] = jnp.where(first, a, b)
        out_ref[:, :, head:] = jnp.where(first, b, a)
        total = refs[0][...]
        for ref in refs[1:number]:
            total = total + ref[...]
        router_out[...] = total

    return pl.pallas_call(
        body,
        grid_spec=pltpu.PrefetchScalarGridSpec(
            num_scalar_prefetch=1,
            grid=(1,),
            in_specs=[whole(mine.shape)] * 2 + [whole(routers[0].shape)] * number,
            out_specs=[whole((2, slots, 2 * head)), whole(routers[0].shape)],
        ),
        out_shape=[
            jax.ShapeDtypeStruct((2, slots, 2 * head), BF16),
            jax.ShapeDtypeStruct(routers[0].shape, F32),
        ],
        compiler_params=pltpu.CompilerParams(vmem_limit_bytes=16 << 20),
        name="finish",
    )(core, mine, taken, *routers)


def shards(hidden, queries, keys_values, w_router, routed, counts, grad_out):
    seq = lax.axis_size("seq")
    tp = lax.axis_size("tp")
    slots = routed.shape[1]
    kv_local = keys_values.shape[2] // HEAD_WIDTH
    q_local = queries.shape[1] // HEAD_WIDTH
    group = q_local // kv_local
    split = 2 if kv_local == 2 else 1
    wide = -(-slots // LANES) * LANES
    if kv_local != split or seq & (seq - 1) or slots % 32 or group * 32 % LANES:
        raise ValueError("unsupported sizes")
    plan = Plan(seq, split, slots, group, wide)
    own = lax.axis_index("seq").astype(jnp.int32)
    shard = own.reshape(1)
    core = (own % 2).reshape(1)

    def across(value, k):
        return lax.ppermute(value, "seq", [(i, i ^ k) for i in range(seq)])

    def around(value, k):
        return lax.ppermute(value, "tp", [(i, (i + k) % tp) for i in range(tp)])

    far_first = sorted(range(split, seq, split), key=lambda k: -bin(k).count("1"))

    *sent, chosen_x, logit_part = gather_first(
        keys_values, hidden, w_router, routed, core, split, wide
    )
    block = jnp.stack([sent[0]] + [across(part, 1) for part in sent[1:]])
    arrived = {k: across(block, k) for k in far_first}
    blocks = [block] + [arrived[k] for k in range(split, seq, split)]
    logit = logit_part
    if split == 2:
        logit = jnp.concatenate([logit_part, across(logit_part, 1)], axis=0)
    logits = [logit] + [around(logit, k) for k in range(1, tp)]
    rows = [chosen_x] + [across(chosen_x, 1)] * (split - 1)
    parts = gather_queries(queries, routed, grad_out, core, split, [block, logit])
    sides = [parts[0]] + [across(part, 1) for part in parts[1:]]

    results = attend(plan, shard, counts, blocks, sides, logits)
    outs, backs, gate = results[:split], results[split:-1], results[-1]
    gates = [gate] + [around(gate, k) for k in range(1, tp)]
    returned = {k: across(backs[k // split], k) for k in far_first}
    if split == 1:
        branch_out, grad_queries = outs[0][0], outs[0][1]
    else:
        taken = across(outs[1], 1)
        branch_out, grad_queries = join_halves(core, outs[0], taken)
    router = router_part(shard, counts, logits, gates, rows, wide, [branch_out])
    if split == 2:
        router = router + across(router, 1)
    routers = [router] + [across(router, k) for k in far_first]
    sums = add_up([backs[0]] + [returned[k] for k in far_first], [router])
    if split == 1:
        grad_keys_values, grad_router = sums[0], sum(routers)
    else:
        grad_keys_values, grad_router = finish(core, sums[0], across(sums[1], 1), routers)
    return (branch_out, grad_queries, grad_keys_values, grad_router.reshape(-1))


def solution(mesh):
    in_specs = (
        P("seq", "tp"),
        P("seq", "tp"),
        P(None, "seq", "tp"),
        P("tp"),
        P("seq", None),
        P(),
        P("seq", "tp"),
    )
    out_specs = (P("seq", "tp"), P("seq", "tp"), P(None, "seq", "tp"), P("tp"))

    return jax.shard_map(shards, mesh=mesh, in_specs=in_specs, out_specs=out_specs, check_vma=False)
```

profile of v0, /device:TPU:0, one launch (start us, length us, event | category | flops | bytes accessed | tf_op | source)
XLA Modules:
  0.0 71.3 jit_solution(1674956787687834754)
XLA Ops:
  0.6 0.0 copy-start.4
  0.6 0.0 copy-start.1
  0.7 0.0 copy-start
  0.7 0.0 copy-start.5
  0.7 6.1 %gather_first.1 = (bf16[2,160,128]{2,1,0:T(8,128)(2,1)}, bf16[2,160,128]{2,1,0:T(8,128)(2,1)}, bf16[160,2048]{1,0:T(8,128)(2,1)}, f32[1,256]{1,0:T(1,128)}) custom-call(s32[1]{0:T(128)} %bitcast.core_ref, s32[1,160]{1,0:T(1,128)} %routed_ref.3, bf16[16,128]{1,0:T(8,128)(2,1)} %bitcast.8, bf16[2,1280,256]{2,1,0:T(8,128)(2,1)} %kv_hbm.1, bf16[1280,2048]{1,0:T(8,128)(2,1)} %x_hbm.1), custom_call_target="tpu_custom_call" | custom-call | tf_op jit(solution)/shard_map/gather_first/pallas_call | solution.py:96
  6.8 0.0 copy-start.2
  6.8 0.6 collective-permute-start.4
  7.4 0.1 collective-permute-start
  7.5 1.0 %collective-permute-done.4 = f32[1,256]{1,0:T(1,128)S(1)} collective-permute-done((f32[1,256]{1,0:T(1,128)}, f32[1,256]{1,0:T(1,128)S(1)}, u32[]{:S(2)}, u32[]{:S(2)}) %collective-permute-start.4) | collective-permute-done | bytes 1056 | tf_op jit(solution)/shard_map/ppermute | solution.py:606
  8.4 0.7 pad_maximum_fusion.1.refs_1_.refs_6_.refs_0_
  9.1 0.0 collective-permute-done
  9.1 0.9 %pad_maximum_fusion.refs_0_ = bf16[2,2,160,128]{3,2,1,0:T(8,128)(2,1)S(1)} fusion(bf16[1,2,160,128]{3,2,1,0:T(8,128)(2,1)S(1)} %bitcast.7, bf16[1,2,160,128]{3,2,1,0:T(8,128)(2,1)} %bitcast.6), kind=kLoop, calls=%fused_computation | loop fusion | flops 81920 | bytes 327680 | tf_op jit(solution)/shard_map/stack | solution.py:616
  10.0 0.0 copy-done.4
  10.0 0.0 copy-done.1
  10.1 0.0 copy-done
  10.1 2.0 %gather_queries.1 = (bf16[2,160,1024]{2,1,0:T(8,128)(2,1)S(1)}, bf16[2,160,1024]{2,1,0:T(8,128)(2,1)S(1)}) custom-call(s32[1]{0:T(128)} %bitcast.core_ref, s32[1,160]{1,0:T(1,128)S(1)} %copy-done.4, bf16[160,2048]{1,0:T(8,128)(2,1)S(1)} %copy-done.1, bf16[1280,2048]{1,0:T(8,128)(2,1)S(1)} %copy-done, bf16[2,2,160,128]{3,2,1,0:T(8,128)(2,1)S(1)} %pad_maximum_fusion.refs_0_, ...), custom_call_target="tpu_custom_call" | custom-call | tf_op jit(solution)/shard_map/gather_queries/pallas_call | solution.py:172
  12.1 0.4 collective-permute-start.5
  12.5 2.6 %collective-permute-start.1 = (bf16[2,2,160,128]{3,2,1,0:T(8,128)(2,1)S(1)}, bf16[2,2,160,128]{3,2,1,0:T(8,128)(2,1)S(1)}, u32[]{:S(2)}, u32[]{:S(2)}) collective-permute-start(bf16[2,2,160,128]{3,2,1,0:T(8,128)(2,1)S(1)} %pad_maximum_fusion.refs_0_), channel_id=1, source_target_pairs={{0,8},{4,12},{8,0},{12,4},{16,24},{20,28},{24,16},{28,20},{1,9},{5... | collective-permute-start | bytes 491528 | tf_op jit(solution)/shard_map/ppermute | solution.py:606
  15.1 1.5 %collective-permute-start.2 = (bf16[2,2,160,128]{3,2,1,0:T(8,128)(2,1)S(1)}, bf16[2,2,160,128]{3,2,1,0:T(8,128)(2,1)S(1)}, u32[]{:S(2)}, u32[]{:S(2)}) collective-permute-start(bf16[2,2,160,128]{3,2,1,0:T(8,128)(2,1)S(1)} %pad_maximum_fusion.refs_0_), channel_id=1, source_target_pairs={{0,16},{4,20},{8,24},{12,28},{16,0},{20,4},{24,8},{28,12},{1,17},{... | collective-permute-start | bytes 491528 | tf_op jit(solution)/shard_map/ppermute | solution.py:606
  16.6 0.0 collective-permute-start.3
  16.6 2.0 %collective-permute-start.6 = (f32[2,256]{1,0:T(2,128)S(1)}, f32[2,256]{1,0:T(2,128)S(1)}, u32[]{:S(2)}, u32[]{:S(2)}) collective-permute-start(f32[2,256]{1,0:T(2,128)S(1)} %pad_maximum_fusion.1.refs_1_.refs_6_.refs_0_), channel_id=1, source_target_pairs={{0,1},{1,2},{2,3},{3,0},{4,5},{5,6},{6,7},{7,4},{8,9},{9,10},{10,1... | collective-permute-start | bytes 6152 | tf_op jit(solution)/shard_map/ppermute | solution.py:609
  18.7 3.6 %collective-permute-done.6.refs_7_.refs_1_ = f32[2,256]{1,0:T(2,128)S(1)} collective-permute-done((f32[2,256]{1,0:T(2,128)S(1)}, f32[2,256]{1,0:T(2,128)S(1)}, u32[]{:S(2)}, u32[]{:S(2)}) %collective-permute-start.6) | collective-permute-done | bytes 2080 | tf_op jit(solution)/shard_map/ppermute | solution.py:609
  22.3 1.0 %collective-permute-start.7 = (f32[2,256]{1,0:T(2,128)S(1)}, f32[2,256]{1,0:T(2,128)S(1)}, u32[]{:S(2)}, u32[]{:S(2)}) collective-permute-start(f32[2,256]{1,0:T(2,128)S(1)} %pad_maximum_fusion.1.refs_1_.refs_6_.refs_0_), channel_id=1, source_target_pairs={{0,2},{1,3},{2,0},{3,1},{4,6},{5,7},{6,4},{7,5},{8,10},{9,11},{10,... | collective-permute-start | bytes 6152 | tf_op jit(solution)/shard_map/ppermute | solution.py:609
  23.3 3.5 %collective-permute-done.7.refs_8_.refs_2_ = f32[2,256]{1,0:T(2,128)S(1)} collective-permute-done((f32[2,256]{1,0:T(2,128)S(1)}, f32[2,256]{1,0:T(2,128)S(1)}, u32[]{:S(2)}, u32[]{:S(2)}) %collective-permute-start.7) | collective-permute-done | bytes 2080 | tf_op jit(solution)/shard_map/ppermute | solution.py:609
  26.8 2.0 %collective-permute-start.8 = (f32[2,256]{1,0:T(2,128)S(1)}, f32[2,256]{1,0:T(2,128)S(1)}, u32[]{:S(2)}, u32[]{:S(2)}) collective-permute-start(f32[2,256]{1,0:T(2,128)S(1)} %pad_maximum_fusion.1.refs_1_.refs_6_.refs_0_), channel_id=1, source_target_pairs={{0,3},{1,0},{2,1},{3,2},{4,7},{5,4},{6,5},{7,6},{8,11},{9,8},{10,9... | collective-permute-start | bytes 6152 | tf_op jit(solution)/shard_map/ppermute | solution.py:609
  28.8 1.6 %collective-permute-done.8.refs_9_.refs_3_ = f32[2,256]{1,0:T(2,128)S(1)} collective-permute-done((f32[2,256]{1,0:T(2,128)S(1)}, f32[2,256]{1,0:T(2,128)S(1)}, u32[]{:S(2)}, u32[]{:S(2)}) %collective-permute-start.8) | collective-permute-done | bytes 2080 | tf_op jit(solution)/shard_map/ppermute | solution.py:609
  30.3 0.0 copy-done.2
  30.3 0.0 collective-permute-start.16
  30.3 0.0 collective-permute-done.1.refs_1_
  30.4 0.0 collective-permute-done.2.refs_2_
  30.4 0.0 collective-permute-done.3.refs_3_
  30.4 0.0 collective-permute-done.5.refs_5_
  30.4 0.0 copy-done.5
  30.4 8.0 %attend.1 = (bf16[2,160,1024]{2,1,0:T(8,128)(2,1)S(1)}, bf16[2,160,1024]{2,1,0:T(8,128)(2,1)S(1)}, bf16[2,2,160,128]{3,2,1,0:T(8,128)(2,1)S(1)}, bf16[2,2,160,12...) custom-call(s32[1]{0:T(128)} %bitcast.1.shard_ref, ...), custom_call_target="tpu_custom_call" | custom-call | tf_op jit(solution)/shard_map/attend/pallas_call | solution.py:423
  38.4 0.6 collective-permute-start.9
  39.0 11.0 %collective-permute-start.10 = (bf16[2,2,160,128]{3,2,1,0:T(8,128)(2,1)S(1)}, bf16[2,2,160,128]{3,2,1,0:T(8,128)(2,1)S(1)}, u32[]{:S(2)}, u32[]{:S(2)}) collective-permute-start(bf16[2,2,160,128]{3,2,1,0:T(8,128)(2,1)S(1)} %get-tuple-element.33), channel_id=1, source_target_pairs={{0,24},{4,28},{8,16},{12,20},{16,8},{20,12},{24,0},{28,4},{1,25},{... | collective-permute-start | bytes 491528 | tf_op jit(solution)/shard_map/ppermute | solution.py:606
  50.0 0.0 collective-permute-start.11
  50.0 0.6 collective-permute-start.12
  50.6 0.0 collective-permute-done.16.refs_9_
  50.6 0.0 collective-permute-start.13
  50.6 5.4 %collective-permute-done.13.refs_5_ = f32[2,256]{1,0:T(2,128)S(1)} collective-permute-done((f32[2,256]{1,0:T(2,128)S(1)}, f32[2,256]{1,0:T(2,128)S(1)}, u32[]{:S(2)}, u32[]{:S(2)}) %collective-permute-start.13) | collective-permute-done | bytes 2080 | tf_op jit(solution)/shard_map/ppermute | solution.py:609
  55.9 0.1 collective-permute-start.14
  56.0 0.0 collective-permute-done.9.taken_ref
  56.0 1.7 %collective-permute-start.15 = (f32[2,256]{1,0:T(2,128)S(1)}, f32[2,256]{1,0:T(2,128)S(1)}, u32[]{:S(2)}, u32[]{:S(2)}) collective-permute-start(f32[2,256]{1,0:T(2,128)S(1)} %get-tuple-element.36.refs_4_), channel_id=1, source_target_pairs={{0,3},{1,0},{2,1},{3,2},{4,7},{5,4},{6,5},{7,6},{8,11},{9,8},{10,9... | collective-permute-start | bytes 6152 | tf_op jit(solution)/shard_map/ppermute | solution.py:609
  57.7 1.1 %join_halves.1 = (bf16[160,2048]{1,0:T(8,128)(2,1)}, bf16[160,2048]{1,0:T(8,128)(2,1)}) custom-call(s32[1]{0:T(128)} %bitcast.core_ref, bf16[2,160,1024]{2,1,0:T(8,128)(2,1)S(1)} %get-tuple-element.28.mine_ref, bf16[2,160,1024]{2,1,0:T(8,128)(2,1)S(1)} %collective-permute-done.9.taken_ref), custom_call_target="tpu_custom_call" | custom-call | tf_op jit(solution)/shard_map/join_halves/pallas_call | solution.py:518
  58.9 1.6 %collective-permute-done.14.refs_6_ = f32[2,256]{1,0:T(2,128)S(1)} collective-permute-done((f32[2,256]{1,0:T(2,128)S(1)}, f32[2,256]{1,0:T(2,128)S(1)}, u32[]{:S(2)}, u32[]{:S(2)}) %collective-permute-start.14) | collective-permute-done | bytes 2080 | tf_op jit(solution)/shard_map/ppermute | solution.py:609
  60.4 0.0 collective-permute-done.15.refs_7_
  60.4 1.1 %copy-done.3 = bf16[160,2048]{1,0:T(8,128)(2,1)S(1)} copy-done((bf16[160,2048]{1,0:T(8,128)(2,1)S(1)}, bf16[160,2048]{1,0:T(8,128)(2,1)}, u32[]{:S(2)}) %copy-start.3) | copy-done | bytes 655384
  61.5 0.9 %router_part.1 = f32[16,128]{1,0:T(8,128)S(1)} custom-call(s32[1]{0:T(128)} %bitcast.1.shard_ref, s32[8]{0:T(128)S(1)} %copy-done.5, f32[2,256]{1,0:T(2,128)S(1)} %pad_maximum_fusion.1.refs_1_.refs_6_.refs_0_, f32[2,256]{1,0:T(2,128)S(1)} %collective-permute-done.6.refs_7_.refs_1_, f32[2,256]{1,0:T(2,128)S(1)} %collective-permute-done.7.refs_8_.refs_2_, ...), custom_call_target="tpu_custom_call" | custom-call | tf_op jit(solution)/shard_map/router_part/pallas_call | solution.py:489
  62.4 0.1 collective-permute-start.17
  62.5 1.2 %collective-permute-done.17 = f32[16,128]{1,0:T(8,128)S(1)} collective-permute-done((f32[16,128]{1,0:T(8,128)S(1)}, f32[16,128]{1,0:T(8,128)S(1)}, u32[]{:S(2)}, u32[]{:S(2)}) %collective-permute-start.17) | collective-permute-done | bytes 8224 | tf_op jit(solution)/shard_map/ppermute | solution.py:606
  63.7 0.0 collective-permute-done.10.refs_1_
  63.7 0.0 collective-permute-done.11.refs_2_
  63.7 0.0 collective-permute-done.12.refs_3_
  63.7 0.1 add_up.1
  63.8 0.2 collective-permute-start.18
  64.0 2.9 %collective-permute-start.19 = (f32[16,128]{1,0:T(8,128)S(1)}, f32[16,128]{1,0:T(8,128)S(1)}, u32[]{:S(2)}, u32[]{:S(2)}) collective-permute-start(f32[16,128]{1,0:T(8,128)S(1)} %add.8.refs_4_.refs_0_), channel_id=1, source_target_pairs={{0,24},{4,28},{8,16},{12,20},{16,8},{20,12},{24,0},{28,4},{1,25},{... | collective-permute-start | bytes 24584 | tf_op jit(solution)/shard_map/ppermute | solution.py:606
  66.9 0.0 collective-permute-start.20
  66.9 0.6 collective-permute-start.21
  67.5 1.1 %collective-permute-done.19.refs_1_ = f32[16,128]{1,0:T(8,128)S(1)} collective-permute-done((f32[16,128]{1,0:T(8,128)S(1)}, f32[16,128]{1,0:T(8,128)S(1)}, u32[]{:S(2)}, u32[]{:S(2)}) %collective-permute-start.19) | collective-permute-done | bytes 8224 | tf_op jit(solution)/shard_map/ppermute | solution.py:606
  68.6 2.0 %collective-permute-done.20.refs_2_ = f32[16,128]{1,0:T(8,128)S(1)} collective-permute-done((f32[16,128]{1,0:T(8,128)S(1)}, f32[16,128]{1,0:T(8,128)S(1)}, u32[]{:S(2)}, u32[]{:S(2)}) %collective-permute-start.20) | collective-permute-done | bytes 8224 | tf_op jit(solution)/shard_map/ppermute | solution.py:606
  70.6 0.0 collective-permute-done.21.refs_3_
  70.6 0.0 collective-permute-done.18.taken_ref
  70.6 0.7 finish.1
  (2 shorter events, 0.0 us)
Async XLA Ops:
  0.6 9.4 %copy-start.4 = (s32[1,160]{1,0:T(1,128)S(1)}, s32[1,160]{1,0:T(1,128)}, u32[]{:S(2)}) copy-start(s32[1,160]{1,0:T(1,128)} %routed_ref.3) | copy-start | bytes 1924
  0.6 9.4 %copy-start.1 = (bf16[160,2048]{1,0:T(8,128)(2,1)S(1)}, bf16[160,2048]{1,0:T(8,128)(2,1)}, u32[]{:S(2)}) copy-start(bf16[160,2048]{1,0:T(8,128)(2,1)} %g_hbm.1) | copy-start | bytes 1966084
  0.7 9.4 %copy-start = (bf16[1280,2048]{1,0:T(8,128)(2,1)S(1)}, bf16[1280,2048]{1,0:T(8,128)(2,1)}, u32[]{:S(2)}) copy-start(bf16[1280,2048]{1,0:T(8,128)(2,1)} %q_hbm.1) | copy-start | bytes 15728644
  0.7 29.7 %copy-start.5 = (s32[8]{0:T(128)S(1)}, s32[8]{0:T(128)}, u32[]{:S(2)}) copy-start(s32[8]{0:T(128)} %counts_ref.3) | copy-start | bytes 100
  6.8 23.5 %copy-start.2 = (bf16[160,2048]{1,0:T(8,128)(2,1)S(1)}, bf16[160,2048]{1,0:T(8,128)(2,1)}, u32[]{:S(2)}) copy-start(bf16[160,2048]{1,0:T(8,128)(2,1)} %get-tuple-element.37.refs_8_) | copy-start | bytes 1966084
  6.8 1.6 %collective-permute-start.4 = (f32[1,256]{1,0:T(1,128)}, f32[1,256]{1,0:T(1,128)S(1)}, u32[]{:S(2)}, u32[]{:S(2)}) collective-permute-start(f32[1,256]{1,0:T(1,128)} %get-tuple-element.25), channel_id=1, source_target_pairs={{0,4},{4,0},{8,12},{12,8},{16,20},{20,16},{24,28},{28,24},{1,5},{5... | collective-permute-start | bytes 3080 | tf_op jit(solution)/shard_map/ppermute | solution.py:606
  7.4 1.7 %collective-permute-start = (bf16[2,160,128]{2,1,0:T(8,128)(2,1)}, bf16[2,160,128]{2,1,0:T(8,128)(2,1)S(1)}, u32[]{:S(2)}, u32[]{:S(2)}) collective-permute-start(bf16[2,160,128]{2,1,0:T(8,128)(2,1)} %get-tuple-element.24), channel_id=1, source_target_pairs={{0,4},{4,0},{8,12},{12,8},{16,20},{20,16},{24,28},{28,24},{1,5},{5... | collective-permute-start | bytes 245768 | tf_op jit(solution)/shard_map/ppermute | solution.py:606
  12.1 18.3 %collective-permute-start.5 = (bf16[2,160,1024]{2,1,0:T(8,128)(2,1)S(1)}, bf16[2,160,1024]{2,1,0:T(8,128)(2,1)S(1)}, u32[]{:S(2)}, u32[]{:S(2)}) collective-permute-start(bf16[2,160,1024]{2,1,0:T(8,128)(2,1)S(1)} %get-tuple-element.27), channel_id=1, source_target_pairs={{0,4},{4,0},{8,12},{12,8},{16,20},{20,16},{24,28},{28,24},{1,5},{5... | collective-permute-start | bytes 1966088 | tf_op jit(solution)/shard_map/ppermute | solution.py:606
  12.5 17.9 %collective-permute-start.1 = (bf16[2,2,160,128]{3,2,1,0:T(8,128)(2,1)S(1)}, bf16[2,2,160,128]{3,2,1,0:T(8,128)(2,1)S(1)}, u32[]{:S(2)}, u32[]{:S(2)}) collective-permute-start(bf16[2,2,160,128]{3,2,1,0:T(8,128)(2,1)S(1)} %pad_maximum_fusion.refs_0_), channel_id=1, source_target_pairs={{0,8},{4,12},{8,0},{12,4},{16,24},{20,28},{24,16},{28,20},{1,9},{5... | collective-permute-start | bytes 491528 | tf_op jit(solution)/shard_map/ppermute | solution.py:606
  15.1 15.2 %collective-permute-start.2 = (bf16[2,2,160,128]{3,2,1,0:T(8,128)(2,1)S(1)}, bf16[2,2,160,128]{3,2,1,0:T(8,128)(2,1)S(1)}, u32[]{:S(2)}, u32[]{:S(2)}) collective-permute-start(bf16[2,2,160,128]{3,2,1,0:T(8,128)(2,1)S(1)} %pad_maximum_fusion.refs_0_), channel_id=1, source_target_pairs={{0,16},{4,20},{8,24},{12,28},{16,0},{20,4},{24,8},{28,12},{1,17},{... | collective-permute-start | bytes 491528 | tf_op jit(solution)/shard_map/ppermute | solution.py:606
  16.6 13.7 %collective-permute-start.3 = (bf16[2,2,160,128]{3,2,1,0:T(8,128)(2,1)S(1)}, bf16[2,2,160,128]{3,2,1,0:T(8,128)(2,1)S(1)}, u32[]{:S(2)}, u32[]{:S(2)}) collective-permute-start(bf16[2,2,160,128]{3,2,1,0:T(8,128)(2,1)S(1)} %pad_maximum_fusion.refs_0_), channel_id=1, source_target_pairs={{0,24},{4,28},{8,16},{12,20},{16,8},{20,12},{24,0},{28,4},{1,25},{... | collective-permute-start | bytes 491528 | tf_op jit(solution)/shard_map/ppermute | solution.py:606
  16.6 5.6 %collective-permute-start.6 = (f32[2,256]{1,0:T(2,128)S(1)}, f32[2,256]{1,0:T(2,128)S(1)}, u32[]{:S(2)}, u32[]{:S(2)}) collective-permute-start(f32[2,256]{1,0:T(2,128)S(1)} %pad_maximum_fusion.1.refs_1_.refs_6_.refs_0_), channel_id=1, source_target_pairs={{0,1},{1,2},{2,3},{3,0},{4,5},{5,6},{6,7},{7,4},{8,9},{9,10},{10,1... | collective-permute-start | bytes 6152 | tf_op jit(solution)/shard_map/ppermute | solution.py:609
  22.3 4.5 %collective-permute-start.7 = (f32[2,256]{1,0:T(2,128)S(1)}, f32[2,256]{1,0:T(2,128)S(1)}, u32[]{:S(2)}, u32[]{:S(2)}) collective-permute-start(f32[2,256]{1,0:T(2,128)S(1)} %pad_maximum_fusion.1.refs_1_.refs_6_.refs_0_), channel_id=1, source_target_pairs={{0,2},{1,3},{2,0},{3,1},{4,6},{5,7},{6,4},{7,5},{8,10},{9,11},{10,... | collective-permute-start | bytes 6152 | tf_op jit(solution)/shard_map/ppermute | solution.py:609
  26.8 3.6 %collective-permute-start.8 = (f32[2,256]{1,0:T(2,128)S(1)}, f32[2,256]{1,0:T(2,128)S(1)}, u32[]{:S(2)}, u32[]{:S(2)}) collective-permute-start(f32[2,256]{1,0:T(2,128)S(1)} %pad_maximum_fusion.1.refs_1_.refs_6_.refs_0_), channel_id=1, source_target_pairs={{0,3},{1,0},{2,1},{3,2},{4,7},{5,4},{6,5},{7,6},{8,11},{9,8},{10,9... | collective-permute-start | bytes 6152 | tf_op jit(solution)/shard_map/ppermute | solution.py:609
  30.3 20.2 %collective-permute-start.16 = (bf16[160,2048]{1,0:T(8,128)(2,1)S(1)}, bf16[160,2048]{1,0:T(8,128)(2,1)S(1)}, u32[]{:S(2)}, u32[]{:S(2)}) collective-permute-start(bf16[160,2048]{1,0:T(8,128)(2,1)S(1)} %copy-done.2), channel_id=1, source_target_pairs={{0,4},{4,0},{8,12},{12,8},{16,20},{20,16},{24,28},{28,24},{1,5},{5... | collective-permute-start | bytes 1966088 | tf_op jit(solution)/shard_map/ppermute | solution.py:606
  38.4 17.6 %collective-permute-start.9 = (bf16[2,160,1024]{2,1,0:T(8,128)(2,1)S(1)}, bf16[2,160,1024]{2,1,0:T(8,128)(2,1)S(1)}, u32[]{:S(2)}, u32[]{:S(2)}) collective-permute-start(bf16[2,160,1024]{2,1,0:T(8,128)(2,1)S(1)} %get-tuple-element.29), channel_id=1, source_target_pairs={{0,4},{4,0},{8,12},{12,8},{16,20},{20,16},{24,28},{28,24},{1,5},{5... | collective-permute-start | bytes 1966088 | tf_op jit(solution)/shard_map/ppermute | solution.py:606
  39.0 24.7 %collective-permute-start.10 = (bf16[2,2,160,128]{3,2,1,0:T(8,128)(2,1)S(1)}, bf16[2,2,160,128]{3,2,1,0:T(8,128)(2,1)S(1)}, u32[]{:S(2)}, u32[]{:S(2)}) collective-permute-start(bf16[2,2,160,128]{3,2,1,0:T(8,128)(2,1)S(1)} %get-tuple-element.33), channel_id=1, source_target_pairs={{0,24},{4,28},{8,16},{12,20},{16,8},{20,12},{24,0},{28,4},{1,25},{... | collective-permute-start | bytes 491528 | tf_op jit(solution)/shard_map/ppermute | solution.py:606
  50.0 13.7 %collective-permute-start.11 = (bf16[2,2,160,128]{3,2,1,0:T(8,128)(2,1)S(1)}, bf16[2,2,160,128]{3,2,1,0:T(8,128)(2,1)S(1)}, u32[]{:S(2)}, u32[]{:S(2)}) collective-permute-start(bf16[2,2,160,128]{3,2,1,0:T(8,128)(2,1)S(1)} %get-tuple-element.34), channel_id=1, source_target_pairs={{0,8},{4,12},{8,0},{12,4},{16,24},{20,28},{24,16},{28,20},{1,9},{5... | collective-permute-start | bytes 491528 | tf_op jit(solution)/shard_map/ppermute | solution.py:606
  50.0 13.7 %collective-permute-start.12 = (bf16[2,2,160,128]{3,2,1,0:T(8,128)(2,1)S(1)}, bf16[2,2,160,128]{3,2,1,0:T(8,128)(2,1)S(1)}, u32[]{:S(2)}, u32[]{:S(2)}) collective-permute-start(bf16[2,2,160,128]{3,2,1,0:T(8,128)(2,1)S(1)} %get-tuple-element.35), channel_id=1, source_target_pairs={{0,16},{4,20},{8,24},{12,28},{16,0},{20,4},{24,8},{28,12},{1,17},{... | collective-permute-start | bytes 491528 | tf_op jit(solution)/shard_map/ppermute | solution.py:606
  50.6 5.4 %collective-permute-start.13 = (f32[2,256]{1,0:T(2,128)S(1)}, f32[2,256]{1,0:T(2,128)S(1)}, u32[]{:S(2)}, u32[]{:S(2)}) collective-permute-start(f32[2,256]{1,0:T(2,128)S(1)} %get-tuple-element.36.refs_4_), channel_id=1, source_target_pairs={{0,1},{1,2},{2,3},{3,0},{4,5},{5,6},{6,7},{7,4},{8,9},{9,10},{10,1... | collective-permute-start | bytes 6152 | tf_op jit(solution)/shard_map/ppermute | solution.py:609
  55.9 4.5 %collective-permute-start.14 = (f32[2,256]{1,0:T(2,128)S(1)}, f32[2,256]{1,0:T(2,128)S(1)}, u32[]{:S(2)}, u32[]{:S(2)}) collective-permute-start(f32[2,256]{1,0:T(2,128)S(1)} %get-tuple-element.36.refs_4_), channel_id=1, source_target_pairs={{0,2},{1,3},{2,0},{3,1},{4,6},{5,7},{6,4},{7,5},{8,10},{9,11},{10,... | collective-permute-start | bytes 6152 | tf_op jit(solution)/shard_map/ppermute | solution.py:609
  56.0 4.4 %collective-permute-start.15 = (f32[2,256]{1,0:T(2,128)S(1)}, f32[2,256]{1,0:T(2,128)S(1)}, u32[]{:S(2)}, u32[]{:S(2)}) collective-permute-start(f32[2,256]{1,0:T(2,128)S(1)} %get-tuple-element.36.refs_4_), channel_id=1, source_target_pairs={{0,3},{1,0},{2,1},{3,2},{4,7},{5,4},{6,5},{7,6},{8,11},{9,8},{10,9... | collective-permute-start | bytes 6152 | tf_op jit(solution)/shard_map/ppermute | solution.py:609
  60.4 1.1 %copy-start.3 = (bf16[160,2048]{1,0:T(8,128)(2,1)S(1)}, bf16[160,2048]{1,0:T(8,128)(2,1)}, u32[]{:S(2)}) copy-start(bf16[160,2048]{1,0:T(8,128)(2,1)} %get-tuple-element.19.refs_10_) | copy-start | bytes 1966084
  62.4 1.2 %collective-permute-start.17 = (f32[16,128]{1,0:T(8,128)S(1)}, f32[16,128]{1,0:T(8,128)S(1)}, u32[]{:S(2)}, u32[]{:S(2)}) collective-permute-start(f32[16,128]{1,0:T(8,128)S(1)} %router_part.1), channel_id=1, source_target_pairs={{0,4},{4,0},{8,12},{12,8},{16,20},{20,16},{24,28},{28,24},{1,5},{5... | collective-permute-start | bytes 24584 | tf_op jit(solution)/shard_map/ppermute | solution.py:606
  63.8 6.8 %collective-permute-start.18 = (bf16[2,160,128]{2,1,0:T(8,128)(2,1)S(1)}, bf16[2,160,128]{2,1,0:T(8,128)(2,1)S(1)}, u32[]{:S(2)}, u32[]{:S(2)}) collective-permute-start(bf16[2,160,128]{2,1,0:T(8,128)(2,1)S(1)} %get-tuple-element.39), channel_id=1, source_target_pairs={{0,4},{4,0},{8,12},{12,8},{16,20},{20,16},{24,28},{28,24},{1,5},{5... | collective-permute-start | bytes 245768 | tf_op jit(solution)/shard_map/ppermute | solution.py:606
  64.0 4.5 %collective-permute-start.19 = (f32[16,128]{1,0:T(8,128)S(1)}, f32[16,128]{1,0:T(8,128)S(1)}, u32[]{:S(2)}, u32[]{:S(2)}) collective-permute-start(f32[16,128]{1,0:T(8,128)S(1)} %add.8.refs_4_.refs_0_), channel_id=1, source_target_pairs={{0,24},{4,28},{8,16},{12,20},{16,8},{20,12},{24,0},{28,4},{1,25},{... | collective-permute-start | bytes 24584 | tf_op jit(solution)/shard_map/ppermute | solution.py:606
  66.9 3.7 %collective-permute-start.20 = (f32[16,128]{1,0:T(8,128)S(1)}, f32[16,128]{1,0:T(8,128)S(1)}, u32[]{:S(2)}, u32[]{:S(2)}) collective-permute-start(f32[16,128]{1,0:T(8,128)S(1)} %add.8.refs_4_.refs_0_), channel_id=1, source_target_pairs={{0,8},{4,12},{8,0},{12,4},{16,24},{20,28},{24,16},{28,20},{1,9},{5... | collective-permute-start | bytes 24584 | tf_op jit(solution)/shard_map/ppermute | solution.py:606
  66.9 3.7 %collective-permute-start.21 = (f32[16,128]{1,0:T(8,128)S(1)}, f32[16,128]{1,0:T(8,128)S(1)}, u32[]{:S(2)}, u32[]{:S(2)}) collective-permute-start(f32[16,128]{1,0:T(8,128)S(1)} %add.8.refs_4_.refs_0_), channel_id=1, source_target_pairs={{0,16},{4,20},{8,24},{12,28},{16,0},{20,4},{24,8},{28,12},{1,17},{... | collective-permute-start | bytes 24584 | tf_op jit(solution)/shard_map/ppermute | solution.py:606
where the time goes:
time: 71.5 us; the launch traced here: 71.3 us
  starting transfers between devices  28 us (39%)
  waiting for transfers between devices  20.8 us (29%)
  Pallas kernels  18.9 us (26%)
  other arithmetic  1.6 us (2%)
  local copies, waits for them, and re-layouts  1.11 us (2%)
  between operations  0.83 us (1%)
    ppermute x16, starting transfers between devices, across(): return lax.ppermute(value, 'seq', [(i, i ^ k) for i in range(seq)])  21.1 us
    ppermute x6, waiting for transfers between devices, around(): return lax.ppermute(value, 'tp', [(i, (i + k) % tp) for i in range(tp)])  15.6 us
    pallas_call x1, Pallas kernels, attend(): pl.pallas_call(body, grid_spec=pltpu.PrefetchScalarGridSpec(num_scalar_pr...  8.02 us
    ppermute x6, starting transfers between devices, around(): return lax.ppermute(value, 'tp', [(i, (i + k) % tp) for i in range(tp)])  6.89 us
    pallas_call x1, Pallas kernels, gather_first(): pl.pallas_call(body, grid_spec=pltpu.PrefetchScalarGridSpec(num_scalar_pr...  6.14 us
    ppermute x16, waiting for transfers between devices, across(): return lax.ppermute(value, 'seq', [(i, i ^ k) for i in range(seq)])  5.23 us
    pallas_call x1, Pallas kernels, gather_queries(): pl.pallas_call(body, grid_spec=pltpu.PrefetchScalarGridSpec(num_scalar_pr...  1.99 us
  transfers between devices with their start and end apart: 22, of which 9 were waited for; matrix products, arithmetic and copies ran while one was open for 1% of the time, Pallas kernels for 14%

commit v1 on v0

--- a/solution.py
+++ b/solution.py
@@ -50,68 +50,76 @@
     return [jnp.where(first, low, high), jnp.where(first, high, low)]
 
 
-def pieces(rows, number=5):
-    size = -(-rows // number // 16) * 16
-    return [(at, min(size, rows - at)) for at in range(0, rows, size)]
+VMEM = pl.BlockSpec(memory_space=pltpu.VMEM)
+ANYWHERE = pl.BlockSpec(memory_space=pl.ANY)
+SMALL = pltpu.CompilerParams(vmem_limit_bytes=16 << 20)
+
+
+HBM = pl.BlockSpec(memory_space=pltpu.HBM)
+
+
+def in_hbm(*arrays):
+    return [pltpu.with_memory_space_constraint(array, pltpu.HBM) for array in arrays]
 
 
 def gather_first(keys_values, hidden, w_router, routed, core, split, wide):
-    _, tokens, width = keys_values.shape
-    model = hidden.shape[1]
+    tokens, model = hidden.shape
     slots = routed.shape[1]
     step = 256
-    parts = pieces(tokens)
-
-    def body(core_ref, routed_ref, w_ref, kv_hbm, x_hbm, *refs):
-        outs, (x_out, logit_ref, kv_buf, x_buf, acc, kv_sem, x_sem) = refs[:split], refs[split:]
-        kv_copies = [
-            pltpu.make_async_copy(kv_hbm.at[i], kv_buf.at[i], kv_sem.at[i]) for i in range(2)
+    parts = 4 if model % (4 * step) == 0 else 1
+    part = model // parts
+    weights = w_router.reshape(model // LANES, LANES)
+
+    def body(core_ref, routed_hbm, w_hbm, kv_hbm, x_hbm, *refs):
+        outs, (x_out, logit_ref) = refs[:split], refs[split : split + 2]
+        routed_buf, w_buf, kv_buf, x_buf, sem, x_sem = refs[split + 2 :]
+        fetch = pltpu.make_async_copy(routed_hbm, routed_buf, sem.at[2])
+        fetch_w = pltpu.make_async_copy(w_hbm, w_buf, sem.at[3])
+        copies = [
+            pltpu.make_async_copy(kv_hbm.at[i], kv_buf.at[i], sem.at[i]) for i in range(2)
         ]
         x_copies = [
             pltpu.make_async_copy(
-                x_hbm.at[pl.ds(at, size)], x_buf.at[pl.ds(at, size)], x_sem.at[p]
+                x_hbm.at[:, pl.ds(p * part, part)], x_buf.at[:, pl.ds(p * part, part)], x_sem.at[p]
             )
-            for p, (at, size) in enumerate(parts)
+            for p in range(parts)
         ]
-        for copy in kv_copies + x_copies:
+        for copy in [fetch, fetch_w] + copies + x_copies:
             copy.start()
-        select = one_hot(routed_ref[...], tokens)
+        fetch.wait()
+        select = one_hot(routed_buf[...], tokens)
         for i in range(2):
-            kv_copies[i].wait()
+            copies[i].wait()
             rows = dot(select, kv_buf[i]).astype(BF16)
-            for out, part in zip(outs, rows_of(split, core_ref[0], rows)):
-                out[i] = part
-        for copy in x_copies:
-            copy.wait()
-        acc[...] = jnp.zeros_like(acc)
-        for j in range(model // step):
-            rows = dot(select, x_buf[:, j * step : (j + 1) * step])
-            x_out[:, j * step : (j + 1) * step] = rows.astype(BF16)
-            for t in range(step // LANES):
-                b = j * (step // LANES) + t
-                weight = w_ref[b : b + 1, :].astype(F32)
-                acc[...] += rows[:, t * LANES : (t + 1) * LANES] * weight
-        logit_ref[...] = column_to_row(jnp.sum(acc[...], axis=1, keepdims=True), wide)
+            for out, rows_part in zip(outs, rows_of(split, core_ref[0], rows)):
+                out[i] = rows_part
+        fetch_w.wait()
+        acc = jnp.zeros((slots, LANES), F32)
+        for p in range(parts):
+            x_copies[p].wait()
+            for j in range(p * part // step, (p + 1) * part // step):
+                rows = dot(select, x_buf[:, j * step : (j + 1) * step])
+                x_out[:, j * step : (j + 1) * step] = rows.astype(BF16)
+                for t in range(step // LANES):
+                    b = j * (step // LANES) + t
+                    weight = w_buf[b : b + 1, :].astype(F32)
+                    acc = acc + rows[:, t * LANES : (t + 1) * LANES] * weight
+        logit_ref[...] = column_to_row(jnp.sum(acc, axis=1, keepdims=True), wide)
 
     return pl.pallas_call(
         body,
         grid_spec=pltpu.PrefetchScalarGridSpec(
             num_scalar_prefetch=1,
             grid=(1,),
-            in_specs=[
-                whole((1, slots)),
-                whole((model // LANES, LANES)),
-                pl.BlockSpec(memory_space=pltpu.HBM),
-                pl.BlockSpec(memory_space=pltpu.HBM),
-            ],
-            out_specs=[whole((2, slots, HEAD_WIDTH))] * split
-            + [whole((slots, model)), whole((1, wide))],
+            in_specs=[HBM] * 4,
+            out_specs=[VMEM] * (split + 2),
             scratch_shapes=[
-                pltpu.VMEM((2, tokens, width), BF16),
-                pltpu.VMEM((tokens, model), BF16),
-                pltpu.VMEM((slots, LANES), F32),
-                pltpu.SemaphoreType.DMA((2,)),
-                pltpu.SemaphoreType.DMA((len(parts),)),
+                pltpu.VMEM(routed.shape, jnp.int32),
+                pltpu.VMEM(weights.shape, BF16),
+                pltpu.VMEM(keys_values.shape, BF16),
+                pltpu.VMEM(hidden.shape, BF16),
+                pltpu.SemaphoreType.DMA((4,)),
+                pltpu.SemaphoreType.DMA((parts,)),
             ],
         ),
         out_shape=[jax.ShapeDtypeStruct((2, slots, HEAD_WIDTH), BF16)] * split
@@ -119,9 +127,9 @@
             jax.ShapeDtypeStruct((slots, model), BF16),
             jax.ShapeDtypeStruct((1, wide), F32),
         ],
-        compiler_params=pltpu.CompilerParams(vmem_limit_bytes=58 << 20),
+        compiler_params=SMALL,
         name="gather_first",
-    )(core, routed, w_router.reshape(model // LANES, LANES), keys_values, hidden)
+    )(core, *in_hbm(routed, weights, keys_values, hidden))
 
 
 def gather_queries(queries, routed, grad_out, core, split, after):
@@ -129,66 +137,28 @@
     slots = routed.shape[1]
     half = width // split
     step = 256
-    parts = pieces(tokens)
-
-    def body(core_ref, routed_ref, g_hbm, q_hbm, *refs):
-        refs = refs[len(after) :]
-        outs, (g_buf, q_buf, rows_buf, sem, g_sem, out_sem) = refs[:split], refs[split:]
-        copies = [
-            pltpu.make_async_copy(q_hbm.at[pl.ds(at, size)], q_buf.at[pl.ds(at, size)], sem.at[p])
-            for p, (at, size) in enumerate(parts)
-        ]
-        load = pltpu.make_async_copy(g_hbm, g_buf, g_sem)
-        for copy in copies + [load]:
-            copy.start()
+
+    def body(core_ref, routed_ref, g_ref, q_ref, *refs):
+        outs = refs[len(after) :]
         select = one_hot(routed_ref[...], tokens)
-
-        def give(source, kind):
-            for h in range(split):
-                columns = pl.ds(h * half, half)
-                for o in range(split):
-                    copy = pltpu.make_async_copy(
-                        source.at[:, columns], outs[o].at[kind], out_sem.at[kind, h]
-                    )
-                    if split == 1:
-                        copy.start()
-                    else:
-                        pl.when(core_ref[0] == (h ^ o))(copy.start)
-
-        load.wait()
-        give(g_buf, 1)
-        for copy in copies:
-            copy.wait()
-        for j in range(width // step):
-            at = slice(j * step, (j + 1) * step)
-            rows_buf[:, at] = dot(select, q_buf[:, at]).astype(BF16)
-        give(rows_buf, 0)
-        for kind in range(2):
-            for h in range(split):
-                pltpu.make_async_copy(
-                    g_buf.at[:, pl.ds(h * half, half)], outs[0].at[kind], out_sem.at[kind, h]
-                ).wait()
+        for o in range(split):
+            start = pl.multiple_of((core_ref[0] ^ o) % split * half, half)
+            outs[o][1] = g_ref[:, pl.ds(start, half)]
+            for j in range(half // step):
+                at = pl.ds(pl.multiple_of(start + j * step, step), step)
+                rows = dot(select, q_ref[:, at]).astype(BF16)
+                outs[o][0, :, j * step : (j + 1) * step] = rows
 
     return pl.pallas_call(
         body,
         grid_spec=pltpu.PrefetchScalarGridSpec(
             num_scalar_prefetch=1,
             grid=(1,),
-            in_specs=[whole((1, slots))]
-            + [pl.BlockSpec(memory_space=pltpu.HBM)] * 2
-            + [pl.BlockSpec(memory_space=pl.ANY)] * len(after),
-            out_specs=[pl.BlockSpec(memory_space=pl.ANY)] * split,
-            scratch_shapes=[
-                pltpu.VMEM((slots, width), BF16),
-                pltpu.VMEM((tokens, width), BF16),
-                pltpu.VMEM((slots, width), BF16),
-                pltpu.SemaphoreType.DMA((len(parts),)),
-                pltpu.SemaphoreType.DMA,
-                pltpu.SemaphoreType.DMA((2, split)),
-            ],
+            in_specs=[VMEM] * 3 + [ANYWHERE] * len(after),
+            out_specs=[VMEM] * split,
         ),
         out_shape=[jax.ShapeDtypeStruct((2, slots, half), BF16)] * split,
-        compiler_params=pltpu.CompilerParams(vmem_limit_bytes=16 << 20),
+        compiler_params=SMALL,
         name="gather_queries",
     )(core, routed, grad_out, queries, *after)
 
@@ -211,10 +181,6 @@
     )
 
 
-def whole(shape):
-    return pl.BlockSpec(shape, lambda *_: (0,) * len(shape))
-
-
 def total_of(refs, side):
     total = refs[0][side : side + 1, :]
     for ref in refs[1:]:
@@ -244,18 +210,13 @@
     def body(shard_ref, counts_ref, *refs):
         refs = list(refs)
         block_refs = [refs.pop(0) for _ in range(plan.blocks)]
-        side_hbm = [refs.pop(0) for _ in range(split)]
+        side_refs = [refs.pop(0) for _ in range(split)]
         logit_refs = [refs.pop(0) for _ in range(len(logits))]
-        out_hbm = [refs.pop(0) for _ in range(split)]
+        out_refs = [refs.pop(0) for _ in range(split)]
         back_refs = [refs.pop(0) for _ in range(plan.blocks)]
         gate_ref = refs.pop(0)
-        (side_buf, out_buf, keys, values, place, keys_t, values_t, scores) = refs[:8]
-        (key_acc, value_acc, columns, gate_column, starts, in_sem, out_sem) = refs[8:]
-        fetch = [
-            pltpu.make_async_copy(side_hbm[i], side_buf.at[i], in_sem.at[i]) for i in range(split)
-        ]
-        for copy in fetch:
-            copy.start()
+        (keys, values, place, keys_t, values_t, scores, pulls) = refs[:7]
+        (key_acc, value_acc, columns, gate_column, starts) = refs[7:]
         own = shard_ref[0]
         end = jnp.int32(0)
         for j in range(seq):
@@ -300,26 +261,23 @@
                 at = slice(b * LANES, (b + 1) * LANES)
                 column = row_to_column(weight[:, at], LANES)
                 columns[side, at, :] = jnp.broadcast_to(column, (LANES, LANES))
-        for copy in fetch:
-            copy.wait()
-
-        def chunk_step(u, _):
-            side = u // plan.chunks
+
+        def chunk_step(side, chunk, _):
             mine = own ^ side
             live = counts_ref[mine]
             offset = starts[mine]
-            first = pl.multiple_of((u % plan.chunks) * plan.rows, plan.rows)
+            first = pl.multiple_of(chunk * plan.rows, plan.rows)
             at = pl.ds(first, plan.rows)
             needed = (offset + jnp.minimum(live, first + plan.rows) + tile - 1) // tile
             needed = jnp.where(first < live, needed, 0)
 
             @pl.when(needed == 0)
             def _():
-                out_buf[side, :, at, :] = jnp.zeros((2, plan.rows, width), BF16)
+                out_refs[side][:, at, :] = jnp.zeros((2, plan.rows, width), BF16)
 
             def work(tiles):
-                q = stack_heads(side_buf[side, 0, at, :], plan)
-                upstream = stack_heads(side_buf[side, 1, at, :], plan).astype(F32)
+                q = stack_heads(side_refs[side][0, at, :], plan)
+                upstream = stack_heads(side_refs[side][1, at, :], plan).astype(F32)
                 weight = jnp.concatenate([columns[side, at, :]] * plan.group, axis=0)
                 narrow = (upstream * weight).astype(BF16)
                 q_t = q.T
@@ -338,6 +296,7 @@
                     allowed = jnp.concatenate([place[here, :]] * reps, axis=1) <= positions
                     s = jnp.where(allowed, s, -jnp.inf)
                     scores[here, :] = s
+                    pulls[here, :] = dot(values[here, :], narrow_t)
                     return jnp.maximum(running, jnp.max(s, axis=0, keepdims=True))
 
                 top = repeat(tiles, score, jnp.full((1, lanes), -1e30, F32))
@@ -362,7 +321,7 @@
                 def back(t, grad_t):
                     here = here_of(t)
                     p = scores[here, :] * share
-                    dp = dot(values[here, :], narrow_t)
+                    dp = pulls[here, :]
                     value_acc[here, :] += dot(p.astype(BF16), narrow)
                     ds = (p * (dp - delta)).astype(BF16)
                     key_acc[here, :] += dot(ds, q)
@@ -380,8 +339,8 @@
                 for h in range(plan.group):
                     heads = slice(h * HEAD_WIDTH, (h + 1) * HEAD_WIDTH)
                     rows = slice(h * plan.rows, (h + 1) * plan.rows)
-                    out_buf[side, 0, at, heads] = weighted[rows]
-                    out_buf[side, 1, at, heads] = grad[rows]
+                    out_refs[side][0, at, heads] = weighted[rows]
+                    out_refs[side][1, at, heads] = grad[rows]
 
             if plan.tiles <= 5:
                 for tiles in range(1, plan.tiles + 1):
@@ -390,12 +349,8 @@
                 pl.when(needed > 0)(functools.partial(work, needed))
             return 0
 
-        lax.fori_loop(0, split * plan.chunks, chunk_step, 0)
-        push = [
-            pltpu.make_async_copy(out_buf.at[i], out_hbm[i], out_sem.at[i]) for i in range(split)
-        ]
-        for copy in push:
-            copy.start()
+        for side in range(split):
+            lax.fori_loop(0, plan.chunks, functools.partial(chunk_step, side), 0)
         for side in range(split):
             gate_ref[side : side + 1, :] = column_to_row(
                 jnp.sum(gate_column[side], axis=1, keepdims=True), plan.wide
@@ -415,8 +370,6 @@
                     return 0
 
                 lax.fori_loop(0, (live + 15) // 16, give, 0)
-        for copy in push:
-            copy.wait()
 
     block = (split, 2, slots, HEAD_WIDTH)
     side = (2, slots, width)
@@ -425,28 +378,22 @@
         grid_spec=pltpu.PrefetchScalarGridSpec(
             num_scalar_prefetch=2,
             grid=(1,),
-            in_specs=[whole(block)] * plan.blocks
-            + [pl.BlockSpec(memory_space=pl.ANY)] * split
-            + [whole((split, plan.wide))] * len(logits),
-            out_specs=[pl.BlockSpec(memory_space=pl.ANY)] * split
-            + [whole(block)] * plan.blocks
-            + [whole((split, plan.wide))],
+            in_specs=[VMEM] * plan.blocks
+            + [VMEM] * (split + len(logits)),
+            out_specs=[VMEM] * (split + plan.blocks + 1),
             scratch_shapes=[
-                pltpu.VMEM((split,) + side, BF16),
-                pltpu.VMEM((split,) + side, BF16),
                 pltpu.VMEM((plan.keys + tile, HEAD_WIDTH), BF16),
                 pltpu.VMEM((plan.keys + tile, HEAD_WIDTH), BF16),
                 pltpu.VMEM((plan.keys + tile, LANES), jnp.int32),
                 pltpu.VMEM((HEAD_WIDTH, plan.keys), BF16),
                 pltpu.VMEM((HEAD_WIDTH, plan.keys), BF16),
                 pltpu.VMEM((plan.keys, lanes), F32),
+                pltpu.VMEM((plan.keys, lanes), F32),
                 pltpu.VMEM((plan.keys, HEAD_WIDTH), F32),
                 pltpu.VMEM((plan.keys, HEAD_WIDTH), F32),
                 pltpu.VMEM((split, plan.wide, LANES), F32),
                 pltpu.VMEM((split, slots, LANES), F32),
                 pltpu.SMEM((seq,), jnp.int32),
-                pltpu.SemaphoreType.DMA((split,)),
-                pltpu.SemaphoreType.DMA((split,)),
             ],
         ),
         out_shape=[jax.ShapeDtypeStruct(side, BF16)] * split
@@ -459,7 +406,7 @@
     )(shard, counts, *blocks, *sides, *logits)
 
 
-def router_part(shard, counts, logits, gates, rows, wide, after):
+def router_part(shard, counts, logits, gates, rows):
     slots, width = rows[0].shape
     split = len(rows)
     number = len(logits)
@@ -491,15 +438,13 @@
         grid_spec=pltpu.PrefetchScalarGridSpec(
             num_scalar_prefetch=2,
             grid=(1,),
-            in_specs=[whole((split, wide))] * (2 * number)
-            + [whole((slots, width))] * split
-            + [pl.BlockSpec(memory_space=pl.ANY)] * len(after),
-            out_specs=whole((width // LANES, LANES)),
+            in_specs=[VMEM] * (2 * number + split),
+            out_specs=VMEM,
         ),
         out_shape=jax.ShapeDtypeStruct((width // LANES, LANES), F32),
-        compiler_params=pltpu.CompilerParams(vmem_limit_bytes=16 << 20),
+        compiler_params=SMALL,
         name="router_part",
-    )(shard, counts, *logits, *gates, *rows, *after)
+    )(shard, counts, *logits, *gates, *rows)
 
 
 def join_halves(core, mine, taken):
@@ -520,22 +465,22 @@
         grid_spec=pltpu.PrefetchScalarGridSpec(
             num_scalar_prefetch=1,
             grid=(2,),
-            in_specs=[whole((2, slots, half))] * 2,
+            in_specs=[VMEM] * 2,
             out_specs=[pl.BlockSpec((slots, half), lambda i, c: (0, i ^ c[0]))] * 2,
         ),
         out_shape=[jax.ShapeDtypeStruct((slots, 2 * half), BF16)] * 2,
-        compiler_params=pltpu.CompilerParams(vmem_limit_bytes=16 << 20),
+        compiler_params=SMALL,
         name="join_halves",
     )(core, mine, taken)
 
 
-def add_up(blocks, after):
+def add_up(blocks):
     split = blocks[0].shape[0]
     number = len(blocks)
     shape = blocks[0].shape[1:]
 
     def body(*refs):
-        ins, outs = refs[:number], refs[number + len(after) :]
+        ins, outs = refs[:number], refs[number:]
         for side in range(split):
             acc = ins[0][side].astype(F32)
             for ref in ins[1:]:
@@ -545,13 +490,12 @@
     return pl.pallas_call(
         body,
         grid=(1,),
-        in_specs=[whole(blocks[0].shape)] * number
-        + [pl.BlockSpec(memory_space=pl.ANY)] * len(after),
-        out_specs=[whole(shape)] * split,
+        in_specs=[VMEM] * number,
+        out_specs=[VMEM] * split,
         out_shape=[jax.ShapeDtypeStruct(shape, BF16)] * split,
-        compiler_params=pltpu.CompilerParams(vmem_limit_bytes=16 << 20),
+        compiler_params=SMALL,
         name="add_up",
-    )(*blocks, *after)
+    )(*blocks)
 
 
 def finish(core, mine, taken, routers):
@@ -574,14 +518,14 @@
         grid_spec=pltpu.PrefetchScalarGridSpec(
             num_scalar_prefetch=1,
             grid=(1,),
-            in_specs=[whole(mine.shape)] * 2 + [whole(routers[0].shape)] * number,
-            out_specs=[whole((2, slots, 2 * head)), whole(routers[0].shape)],
+            in_specs=[VMEM] * (2 + number),
+            out_specs=[VMEM] * 2,
         ),
         out_shape=[
             jax.ShapeDtypeStruct((2, slots, 2 * head), BF16),
             jax.ShapeDtypeStruct(routers[0].shape, F32),
         ],
-        compiler_params=pltpu.CompilerParams(vmem_limit_bytes=16 << 20),
+        compiler_params=SMALL,
         name="finish",
     )(core, mine, taken, *routers)
 
@@ -606,7 +550,9 @@
         return lax.ppermute(value, "seq", [(i, i ^ k) for i in range(seq)])
 
     def around(value, k):
-        return lax.ppermute(value, "tp", [(i, (i + k) % tp) for i in range(tp)])
+        if tp & (tp - 1):
+            return lax.ppermute(value, "tp", [(i, (i + k) % tp) for i in range(tp)])
+        return lax.ppermute(value, "tp", [(i, i ^ k) for i in range(tp)])
 
     far_first = sorted(range(split, seq, split), key=lambda k: -bin(k).count("1"))
 
@@ -621,6 +567,7 @@
         logit = jnp.concatenate([logit_part, across(logit_part, 1)], axis=0)
     logits = [logit] + [around(logit, k) for k in range(1, tp)]
     rows = [chosen_x] + [across(chosen_x, 1)] * (split - 1)
+    queries, grad_out, _ = lax.optimization_barrier((queries, grad_out, logit_part))
     parts = gather_queries(queries, routed, grad_out, core, split, [block, logit])
     sides = [parts[0]] + [across(part, 1) for part in parts[1:]]
 
@@ -633,11 +580,11 @@
     else:
         taken = across(outs[1], 1)
         branch_out, grad_queries = join_halves(core, outs[0], taken)
-    router = router_part(shard, counts, logits, gates, rows, wide, [branch_out])
+    router = router_part(shard, counts, logits, gates, rows)
     if split == 2:
         router = router + across(router, 1)
     routers = [router] + [across(router, k) for k in far_first]
-    sums = add_up([backs[0]] + [returned[k] for k in far_first], [router])
+    sums = add_up([backs[0]] + [returned[k] for k in far_first])
     if split == 1:
         grad_keys_values, grad_router = sums[0], sum(routers)
     else:

time: 71.5 us -> 73.4 us (1.027)
  starting transfers between devices: 28 us -> 34.1 us
  Pallas kernels: 18.9 us -> 15.8 us
  waiting for transfers between devices: 20.8 us -> 22.4 us
  other arithmetic: 1.6 us -> 0.03 us
  local copies, waits for them, and re-layouts: 1.11 us -> 0.02 us
    ppermute x16, waiting for transfers between devices: 5.23 us -> 12.6 us  [across(): return lax.ppermute(value, 'seq', [(i, i ^ k) for i in range(seq)])]
    ppermute x6, starting transfers between devices: 6.89 us -> 13.5 us  [around(): return lax.ppermute(value, 'tp', [(i, i ^ k) for i in range(tp)])]
    ppermute x6, waiting for transfers between devices: 15.6 us -> 9.83 us  [around(): return lax.ppermute(value, 'tp', [(i, i ^ k) for i in range(tp)])]
    pallas_call x1, Pallas kernels: 6.14 us -> 4.77 us  [gather_first(): pl.pallas_call(body, grid_spec=pltpu.PrefetchScalarGridSpec(num_scalar_pr...]
    unnamed x12 -> x8, local copies, waits for them, and re-layouts: 1.11 us -> 0.02 us
    another operation x1, other arithmetic: 0.91 us -> 0.02 us  [shards(): block = jnp.stack([sent[0]] + [across(part, 1) for part in sent[1:]])]
    pallas_call x1, Pallas kernels: 8.02 us -> 7.14 us  [attend(): pl.pallas_call(body, grid_spec=pltpu.PrefetchScalarGridSpec(num_scalar_pr...]
    pallas_call x1, Pallas kernels: 1.99 us -> 1.12 us  [gather_queries(): pl.pallas_call(body, grid_spec=pltpu.PrefetchScalarGridSpec(num_scalar_pr...]
  transfers between devices with their start and end apart: 22 -> 22, of which waited for: 9 -> 13; matrix products, arithmetic and copies ran while one was open for 1% -> 0% of each run, Pallas kernels for 14% -> 12%
where the time goes in v1:
time: 73.4 us; the launch traced here: 73.2 us
  starting transfers between devices  34.1 us (46%)
  waiting for transfers between devices  22.4 us (31%)
  Pallas kernels  15.8 us (22%)
  between operations  0.8 us (1%)
    ppermute x16, starting transfers between devices, across(): return lax.ppermute(value, 'seq', [(i, i ^ k) for i in range(seq)])  20.7 us
    ppermute x6, starting transfers between devices, around(): return lax.ppermute(value, 'tp', [(i, i ^ k) for i in range(tp)])  13.5 us
    ppermute x16, waiting for transfers between devices, across(): return lax.ppermute(value, 'seq', [(i, i ^ k) for i in range(seq)])  12.6 us
    ppermute x6, waiting for transfers between devices, around(): return lax.ppermute(value, 'tp', [(i, i ^ k) for i in range(tp)])  9.83 us
    pallas_call x1, Pallas kernels, attend(): pl.pallas_call(body, grid_spec=pltpu.PrefetchScalarGridSpec(num_scalar_pr...  7.14 us
    pallas_call x1, Pallas kernels, gather_first(): pl.pallas_call(body, grid_spec=pltpu.PrefetchScalarGridSpec(num_scalar_pr...  4.77 us
  transfers between devices with their start and end apart: 22, of which 13 were waited for; matrix products, arithmetic and copies ran while one was open for 0% of the time, Pallas kernels for 12%

profile of v1, /device:TPU:0, one launch (start us, length us, event | category | flops | bytes accessed | tf_op | source)
XLA Modules:
  0.0 73.2 jit_solution(13223269345170530333)
XLA Ops:
  0.6 0.0 copy-start.2
  0.6 0.0 copy-start.1
  0.7 0.0 copy-start
  0.7 0.0 copy-start.3
  0.7 4.8 %gather_first.1 = (bf16[2,160,128]{2,1,0:T(8,128)(2,1)S(1)}, bf16[2,160,128]{2,1,0:T(8,128)(2,1)S(1)}, bf16[160,2048]{1,0:T(8,128)(2,1)S(1)}, f32[1,256]{1,0:T(1,128)S(1)}) custom-call(s32[1]{0:T(128)} %bitcast.core_ref, s32[1,160]{1,0:T(1,128)} %routed_ref.1, bf16[16,128]{1,0:T(8,128)(2,1)} %bitcast.8, bf16[2,1280,256]{2,1,0:T(8,128)(2,1)} %kv_hbm.1, ...), custom_call_target="tpu_custom_call" | custom-call | tf_op jit(solution)/shard_map/gather_first/pallas_call | solution.py:109
  5.5 0.6 collective-permute-start.4
  6.0 0.1 collective-permute-start
  6.1 0.7 %collective-permute-done.4 = f32[1,256]{1,0:T(1,128)S(1)} collective-permute-done((f32[1,256]{1,0:T(1,128)S(1)}, f32[1,256]{1,0:T(1,128)S(1)}, u32[]{:S(2)}, u32[]{:S(2)}) %collective-permute-start.4) | collective-permute-done | bytes 1056 | tf_op jit(solution)/shard_map/ppermute | solution.py:550
  6.8 0.4 collective-permute-done
  7.3 0.0 copy-done.2
  7.3 0.0 copy-done.1
  7.3 0.0 copy-done
  7.3 1.1 %gather_queries.1 = (bf16[2,160,1024]{2,1,0:T(8,128)(2,1)S(1)}, bf16[2,160,1024]{2,1,0:T(8,128)(2,1)S(1)}) custom-call(s32[1]{0:T(128)} %bitcast.core_ref, s32[1,160]{1,0:T(1,128)S(1)} %copy-done.2, bf16[160,2048]{1,0:T(8,128)(2,1)S(1)} %copy-done.1, bf16[1280,2048]{1,0:T(8,128)(2,1)S(1)} %copy-done, bf16[2,2,160,128]{3,2,1,0:T(8,128)(2,1)S(1)} %pad_maximum_fusion.refs_0_, ...), custom_call_target="tpu_custom_call" | custom-call | tf_op jit(solution)/shard_map/gather_queries/pallas_call | solution.py:152
  8.5 0.2 collective-permute-start.5
  8.7 2.8 %collective-permute-start.1 = (bf16[2,2,160,128]{3,2,1,0:T(8,128)(2,1)S(1)}, bf16[2,2,160,128]{3,2,1,0:T(8,128)(2,1)S(1)}, u32[]{:S(2)}, u32[]{:S(2)}) collective-permute-start(bf16[2,2,160,128]{3,2,1,0:T(8,128)(2,1)S(1)} %pad_maximum_fusion.refs_0_), channel_id=1, source_target_pairs={{0,8},{4,12},{8,0},{12,4},{16,24},{20,28},{24,16},{28,20},{1,9},{5... | collective-permute-start | bytes 491528 | tf_op jit(solution)/shard_map/ppermute | solution.py:550
  11.5 1.5 %collective-permute-start.2 = (bf16[2,2,160,128]{3,2,1,0:T(8,128)(2,1)S(1)}, bf16[2,2,160,128]{3,2,1,0:T(8,128)(2,1)S(1)}, u32[]{:S(2)}, u32[]{:S(2)}) collective-permute-start(bf16[2,2,160,128]{3,2,1,0:T(8,128)(2,1)S(1)} %pad_maximum_fusion.refs_0_), channel_id=1, source_target_pairs={{0,16},{4,20},{8,24},{12,28},{16,0},{20,4},{24,8},{28,12},{1,17},{... | collective-permute-start | bytes 491528 | tf_op jit(solution)/shard_map/ppermute | solution.py:550
  13.1 0.0 collective-permute-start.3
  13.1 2.1 %collective-permute-start.6 = (f32[2,256]{1,0:T(2,128)S(1)}, f32[2,256]{1,0:T(2,128)S(1)}, u32[]{:S(2)}, u32[]{:S(2)}) collective-permute-start(f32[2,256]{1,0:T(2,128)S(1)} %pad_maximum_fusion.1.refs_1_.refs_6_.refs_0_), channel_id=1, source_target_pairs={{0,1},{1,0},{2,3},{3,2},{4,5},{5,4},{6,7},{7,6},{8,9},{9,8},{10,11... | collective-permute-start | bytes 6152 | tf_op jit(solution)/shard_map/ppermute | solution.py:555
  15.1 1.6 %collective-permute-done.6.refs_7_.refs_1_ = f32[2,256]{1,0:T(2,128)S(1)} collective-permute-done((f32[2,256]{1,0:T(2,128)S(1)}, f32[2,256]{1,0:T(2,128)S(1)}, u32[]{:S(2)}, u32[]{:S(2)}) %collective-permute-start.6) | collective-permute-done | bytes 2080 | tf_op jit(solution)/shard_map/ppermute | solution.py:555
  16.7 3.0 %collective-permute-start.7 = (f32[2,256]{1,0:T(2,128)S(1)}, f32[2,256]{1,0:T(2,128)S(1)}, u32[]{:S(2)}, u32[]{:S(2)}) collective-permute-start(f32[2,256]{1,0:T(2,128)S(1)} %pad_maximum_fusion.1.refs_1_.refs_6_.refs_0_), channel_id=1, source_target_pairs={{0,2},{1,3},{2,0},{3,1},{4,6},{5,7},{6,4},{7,5},{8,10},{9,11},{10,... | collective-permute-start | bytes 6152 | tf_op jit(solution)/shard_map/ppermute | solution.py:555
  19.7 1.6 %collective-permute-done.7.refs_8_.refs_2_ = f32[2,256]{1,0:T(2,128)S(1)} collective-permute-done((f32[2,256]{1,0:T(2,128)S(1)}, f32[2,256]{1,0:T(2,128)S(1)}, u32[]{:S(2)}, u32[]{:S(2)}) %collective-permute-start.7) | collective-permute-done | bytes 2080 | tf_op jit(solution)/shard_map/ppermute | solution.py:555
  21.3 3.9 %collective-permute-start.8 = (f32[2,256]{1,0:T(2,128)S(1)}, f32[2,256]{1,0:T(2,128)S(1)}, u32[]{:S(2)}, u32[]{:S(2)}) collective-permute-start(f32[2,256]{1,0:T(2,128)S(1)} %pad_maximum_fusion.1.refs_1_.refs_6_.refs_0_), channel_id=1, source_target_pairs={{0,3},{1,2},{2,1},{3,0},{4,7},{5,6},{6,5},{7,4},{8,11},{9,10},{10,... | collective-permute-start | bytes 6152 | tf_op jit(solution)/shard_map/ppermute | solution.py:555
  25.2 1.6 %collective-permute-done.8.refs_9_.refs_3_ = f32[2,256]{1,0:T(2,128)S(1)} collective-permute-done((f32[2,256]{1,0:T(2,128)S(1)}, f32[2,256]{1,0:T(2,128)S(1)}, u32[]{:S(2)}, u32[]{:S(2)}) %collective-permute-start.8) | collective-permute-done | bytes 2080 | tf_op jit(solution)/shard_map/ppermute | solution.py:555
  26.8 0.0 collective-permute-start.17
  26.8 0.0 collective-permute-done.1.refs_1_
  26.8 0.0 collective-permute-done.2.refs_2_
  26.8 0.0 collective-permute-done.3.refs_3_
  26.8 0.0 collective-permute-done.5.refs_5_
  26.8 0.0 copy-done.3
  26.8 7.1 %attend.1 = (bf16[2,160,1024]{2,1,0:T(8,128)(2,1)S(1)}, bf16[2,160,1024]{2,1,0:T(8,128)(2,1)S(1)}, bf16[2,2,160,128]{3,2,1,0:T(8,128)(2,1)S(1)}, bf16[2,2,160,12...) custom-call(s32[1]{0:T(128)} %bitcast.1.shard_ref, ...), custom_call_target="tpu_custom_call" | custom-call | tf_op jit(solution)/shard_map/attend/pallas_call | solution.py:376
  34.0 0.6 collective-permute-start.9
  34.5 10.7 %collective-permute-start.10 = (bf16[2,2,160,128]{3,2,1,0:T(8,128)(2,1)S(1)}, bf16[2,2,160,128]{3,2,1,0:T(8,128)(2,1)S(1)}, u32[]{:S(2)}, u32[]{:S(2)}) collective-permute-start(bf16[2,2,160,128]{3,2,1,0:T(8,128)(2,1)S(1)} %get-tuple-element.37), channel_id=1, source_target_pairs={{0,24},{4,28},{8,16},{12,20},{16,8},{20,12},{24,0},{28,4},{1,25},{... | collective-permute-start | bytes 491528 | tf_op jit(solution)/shard_map/ppermute | solution.py:550
  45.2 0.0 collective-permute-start.11
  45.2 0.6 collective-permute-start.12
  45.8 4.5 %collective-permute-done.10.refs_1_ = bf16[2,2,160,128]{3,2,1,0:T(8,128)(2,1)S(1)} collective-permute-done((bf16[2,2,160,128]{3,2,1,0:T(8,128)(2,1)S(1)}, bf16[2,2,160,128]{3,2,1,0:T(8,128)(2,1)S(1)}, u32[]{:S(2)}, u32[]{:S(2)}) %collective-permute-start.10) | collective-permute-done | bytes 163872 | tf_op jit(solution)/shard_map/ppermute | solution.py:550
  50.3 2.2 %collective-permute-done.11.refs_2_ = bf16[2,2,160,128]{3,2,1,0:T(8,128)(2,1)S(1)} collective-permute-done((bf16[2,2,160,128]{3,2,1,0:T(8,128)(2,1)S(1)}, bf16[2,2,160,128]{3,2,1,0:T(8,128)(2,1)S(1)}, u32[]{:S(2)}, u32[]{:S(2)}) %collective-permute-start.11) | collective-permute-done | bytes 163872 | tf_op jit(solution)/shard_map/ppermute | solution.py:550
  52.5 0.7 collective-permute-done.12.refs_3_
  53.2 0.1 add_up.1
  53.3 0.1 collective-permute-start.13
  53.3 0.1 collective-permute-start.14
  53.4 4.1 %collective-permute-start.15 = (f32[2,256]{1,0:T(2,128)S(1)}, f32[2,256]{1,0:T(2,128)S(1)}, u32[]{:S(2)}, u32[]{:S(2)}) collective-permute-start(f32[2,256]{1,0:T(2,128)S(1)} %get-tuple-element.42.refs_4_), channel_id=1, source_target_pairs={{0,2},{1,3},{2,0},{3,1},{4,6},{5,7},{6,4},{7,5},{8,10},{9,11},{10,... | collective-permute-start | bytes 6152 | tf_op jit(solution)/shard_map/ppermute | solution.py:555
  57.6 0.0 collective-permute-done.17.refs_9_
  57.6 0.2 collective-permute-start.16
  57.8 0.0 collective-permute-done.14.refs_5_
  57.8 1.3 %collective-permute-done.15.refs_6_ = f32[2,256]{1,0:T(2,128)S(1)} collective-permute-done((f32[2,256]{1,0:T(2,128)S(1)}, f32[2,256]{1,0:T(2,128)S(1)}, u32[]{:S(2)}, u32[]{:S(2)}) %collective-permute-start.15) | collective-permute-done | bytes 2080 | tf_op jit(solution)/shard_map/ppermute | solution.py:555
  59.1 3.8 %collective-permute-done.16.refs_7_ = f32[2,256]{1,0:T(2,128)S(1)} collective-permute-done((f32[2,256]{1,0:T(2,128)S(1)}, f32[2,256]{1,0:T(2,128)S(1)}, u32[]{:S(2)}, u32[]{:S(2)}) %collective-permute-start.16) | collective-permute-done | bytes 2080 | tf_op jit(solution)/shard_map/ppermute | solution.py:555
  62.9 0.9 %router_part.1 = f32[16,128]{1,0:T(8,128)S(1)} custom-call(s32[1]{0:T(128)} %bitcast.1.shard_ref, s32[8]{0:T(128)S(1)} %copy-done.3, f32[2,256]{1,0:T(2,128)S(1)} %pad_maximum_fusion.1.refs_1_.refs_6_.refs_0_, f32[2,256]{1,0:T(2,128)S(1)} %collective-permute-done.6.refs_7_.refs_1_, f32[2,256]{1,0:T(2,128)S(1)} %collective-permute-done.7.refs_8_.refs_2_, ...), custom_call_target="tpu_custom_call" | custom-call | tf_op jit(solution)/shard_map/router_part/pallas_call | solution.py:436
  63.9 0.1 collective-permute-start.18
  63.9 1.2 %collective-permute-done.18 = f32[16,128]{1,0:T(8,128)S(1)} collective-permute-done((f32[16,128]{1,0:T(8,128)S(1)}, f32[16,128]{1,0:T(8,128)S(1)}, u32[]{:S(2)}, u32[]{:S(2)}) %collective-permute-start.18) | collective-permute-done | bytes 8224 | tf_op jit(solution)/shard_map/ppermute | solution.py:550
  65.1 2.6 %collective-permute-start.19 = (f32[16,128]{1,0:T(8,128)S(1)}, f32[16,128]{1,0:T(8,128)S(1)}, u32[]{:S(2)}, u32[]{:S(2)}) collective-permute-start(f32[16,128]{1,0:T(8,128)S(1)} %add.8.refs_0_), channel_id=1, source_target_pairs={{0,24},{4,28},{8,16},{12,20},{16,8},{20,12},{24,0},{28,4},{1,25},{... | collective-permute-start | bytes 24584 | tf_op jit(solution)/shard_map/ppermute | solution.py:550
  67.7 0.0 collective-permute-start.20
  67.7 0.8 %collective-permute-start.21 = (f32[16,128]{1,0:T(8,128)S(1)}, f32[16,128]{1,0:T(8,128)S(1)}, u32[]{:S(2)}, u32[]{:S(2)}) collective-permute-start(f32[16,128]{1,0:T(8,128)S(1)} %add.8.refs_0_), channel_id=1, source_target_pairs={{0,16},{4,20},{8,24},{12,28},{16,0},{20,4},{24,8},{28,12},{1,17},{... | collective-permute-start | bytes 24584 | tf_op jit(solution)/shard_map/ppermute | solution.py:550
  68.6 1.1 %collective-permute-done.19.refs_1_ = f32[16,128]{1,0:T(8,128)S(1)} collective-permute-done((f32[16,128]{1,0:T(8,128)S(1)}, f32[16,128]{1,0:T(8,128)S(1)}, u32[]{:S(2)}, u32[]{:S(2)}) %collective-permute-start.19) | collective-permute-done | bytes 8224 | tf_op jit(solution)/shard_map/ppermute | solution.py:550
  69.6 1.7 %collective-permute-done.20.refs_2_ = f32[16,128]{1,0:T(8,128)S(1)} collective-permute-done((f32[16,128]{1,0:T(8,128)S(1)}, f32[16,128]{1,0:T(8,128)S(1)}, u32[]{:S(2)}, u32[]{:S(2)}) %collective-permute-start.20) | collective-permute-done | bytes 8224 | tf_op jit(solution)/shard_map/ppermute | solution.py:550
  71.4 0.0 collective-permute-done.21.refs_3_
  71.4 0.0 collective-permute-done.13.taken_ref
  71.4 0.7 finish.1
  72.1 0.0 collective-permute-done.9.taken_ref
  72.1 1.1 %join_halves.1 = (bf16[160,2048]{1,0:T(8,128)(2,1)}, bf16[160,2048]{1,0:T(8,128)(2,1)}) custom-call(s32[1]{0:T(128)} %bitcast.core_ref, bf16[2,160,1024]{2,1,0:T(8,128)(2,1)S(1)} %get-tuple-element.32.mine_ref, bf16[2,160,1024]{2,1,0:T(8,128)(2,1)S(1)} %collective-permute-done.9.taken_ref), custom_call_target="tpu_custom_call" | custom-call | tf_op jit(solution)/shard_map/join_halves/pallas_call | solution.py:463
  (3 shorter events, 0.0 us)
Async XLA Ops:
  0.6 6.7 %copy-start.2 = (s32[1,160]{1,0:T(1,128)S(1)}, s32[1,160]{1,0:T(1,128)}, u32[]{:S(2)}) copy-start(s32[1,160]{1,0:T(1,128)} %routed_ref.1) | copy-start | bytes 1924
  0.6 6.7 %copy-start.1 = (bf16[160,2048]{1,0:T(8,128)(2,1)S(1)}, bf16[160,2048]{1,0:T(8,128)(2,1)}, u32[]{:S(2)}) copy-start(bf16[160,2048]{1,0:T(8,128)(2,1)} %g_ref) | copy-start | bytes 1966084
  0.7 6.7 %copy-start = (bf16[1280,2048]{1,0:T(8,128)(2,1)S(1)}, bf16[1280,2048]{1,0:T(8,128)(2,1)}, u32[]{:S(2)}) copy-start(bf16[1280,2048]{1,0:T(8,128)(2,1)} %q_ref) | copy-start | bytes 15728644
  0.7 26.1 %copy-start.3 = (s32[8]{0:T(128)S(1)}, s32[8]{0:T(128)}, u32[]{:S(2)}) copy-start(s32[8]{0:T(128)} %counts_ref.3) | copy-start | bytes 100
  5.5 1.4 %collective-permute-start.4 = (f32[1,256]{1,0:T(1,128)S(1)}, f32[1,256]{1,0:T(1,128)S(1)}, u32[]{:S(2)}, u32[]{:S(2)}) collective-permute-start(f32[1,256]{1,0:T(1,128)S(1)} %get-tuple-element.27), channel_id=1, source_target_pairs={{0,4},{4,0},{8,12},{12,8},{16,20},{20,16},{24,28},{28,24},{1,5},{5... | collective-permute-start | bytes 3080 | tf_op jit(solution)/shard_map/ppermute | solution.py:550
  6.0 1.3 %collective-permute-start = (bf16[2,160,128]{2,1,0:T(8,128)(2,1)S(1)}, bf16[2,160,128]{2,1,0:T(8,128)(2,1)S(1)}, u32[]{:S(2)}, u32[]{:S(2)}) collective-permute-start(bf16[2,160,128]{2,1,0:T(8,128)(2,1)S(1)} %get-tuple-element.26), channel_id=1, source_target_pairs={{0,4},{4,0},{8,12},{12,8},{16,20},{20,16},{24,28},{28,24},{1,5},{5... | collective-permute-start | bytes 245768 | tf_op jit(solution)/shard_map/ppermute | solution.py:550
  8.5 18.3 %collective-permute-start.5 = (bf16[2,160,1024]{2,1,0:T(8,128)(2,1)S(1)}, bf16[2,160,1024]{2,1,0:T(8,128)(2,1)S(1)}, u32[]{:S(2)}, u32[]{:S(2)}) collective-permute-start(bf16[2,160,1024]{2,1,0:T(8,128)(2,1)S(1)} %get-tuple-element.31), channel_id=1, source_target_pairs={{0,4},{4,0},{8,12},{12,8},{16,20},{20,16},{24,28},{28,24},{1,5},{5... | collective-permute-start | bytes 1966088 | tf_op jit(solution)/shard_map/ppermute | solution.py:550
  8.7 18.1 %collective-permute-start.1 = (bf16[2,2,160,128]{3,2,1,0:T(8,128)(2,1)S(1)}, bf16[2,2,160,128]{3,2,1,0:T(8,128)(2,1)S(1)}, u32[]{:S(2)}, u32[]{:S(2)}) collective-permute-start(bf16[2,2,160,128]{3,2,1,0:T(8,128)(2,1)S(1)} %pad_maximum_fusion.refs_0_), channel_id=1, source_target_pairs={{0,8},{4,12},{8,0},{12,4},{16,24},{20,28},{24,16},{28,20},{1,9},{5... | collective-permute-start | bytes 491528 | tf_op jit(solution)/shard_map/ppermute | solution.py:550
  11.5 15.2 %collective-permute-start.2 = (bf16[2,2,160,128]{3,2,1,0:T(8,128)(2,1)S(1)}, bf16[2,2,160,128]{3,2,1,0:T(8,128)(2,1)S(1)}, u32[]{:S(2)}, u32[]{:S(2)}) collective-permute-start(bf16[2,2,160,128]{3,2,1,0:T(8,128)(2,1)S(1)} %pad_maximum_fusion.refs_0_), channel_id=1, source_target_pairs={{0,16},{4,20},{8,24},{12,28},{16,0},{20,4},{24,8},{28,12},{1,17},{... | collective-permute-start | bytes 491528 | tf_op jit(solution)/shard_map/ppermute | solution.py:550
  13.1 13.7 %collective-permute-start.3 = (bf16[2,2,160,128]{3,2,1,0:T(8,128)(2,1)S(1)}, bf16[2,2,160,128]{3,2,1,0:T(8,128)(2,1)S(1)}, u32[]{:S(2)}, u32[]{:S(2)}) collective-permute-start(bf16[2,2,160,128]{3,2,1,0:T(8,128)(2,1)S(1)} %pad_maximum_fusion.refs_0_), channel_id=1, source_target_pairs={{0,24},{4,28},{8,16},{12,20},{16,8},{20,12},{24,0},{28,4},{1,25},{... | collective-permute-start | bytes 491528 | tf_op jit(solution)/shard_map/ppermute | solution.py:550
  13.1 3.6 %collective-permute-start.6 = (f32[2,256]{1,0:T(2,128)S(1)}, f32[2,256]{1,0:T(2,128)S(1)}, u32[]{:S(2)}, u32[]{:S(2)}) collective-permute-start(f32[2,256]{1,0:T(2,128)S(1)} %pad_maximum_fusion.1.refs_1_.refs_6_.refs_0_), channel_id=1, source_target_pairs={{0,1},{1,0},{2,3},{3,2},{4,5},{5,4},{6,7},{7,6},{8,9},{9,8},{10,11... | collective-permute-start | bytes 6152 | tf_op jit(solution)/shard_map/ppermute | solution.py:555
  16.7 4.6 %collective-permute-start.7 = (f32[2,256]{1,0:T(2,128)S(1)}, f32[2,256]{1,0:T(2,128)S(1)}, u32[]{:S(2)}, u32[]{:S(2)}) collective-permute-start(f32[2,256]{1,0:T(2,128)S(1)} %pad_maximum_fusion.1.refs_1_.refs_6_.refs_0_), channel_id=1, source_target_pairs={{0,2},{1,3},{2,0},{3,1},{4,6},{5,7},{6,4},{7,5},{8,10},{9,11},{10,... | collective-permute-start | bytes 6152 | tf_op jit(solution)/shard_map/ppermute | solution.py:555
  21.3 5.5 %collective-permute-start.8 = (f32[2,256]{1,0:T(2,128)S(1)}, f32[2,256]{1,0:T(2,128)S(1)}, u32[]{:S(2)}, u32[]{:S(2)}) collective-permute-start(f32[2,256]{1,0:T(2,128)S(1)} %pad_maximum_fusion.1.refs_1_.refs_6_.refs_0_), channel_id=1, source_target_pairs={{0,3},{1,2},{2,1},{3,0},{4,7},{5,6},{6,5},{7,4},{8,11},{9,10},{10,... | collective-permute-start | bytes 6152 | tf_op jit(solution)/shard_map/ppermute | solution.py:555
  26.8 30.8 %collective-permute-start.17 = (bf16[160,2048]{1,0:T(8,128)(2,1)S(1)}, bf16[160,2048]{1,0:T(8,128)(2,1)S(1)}, u32[]{:S(2)}, u32[]{:S(2)}) collective-permute-start(bf16[160,2048]{1,0:T(8,128)(2,1)S(1)} %get-tuple-element.43.refs_8_), channel_id=1, source_target_pairs={{0,4},{4,0},{8,12},{12,8},{16,20},{20,16},{24,28},{28,24},{1,5},{5... | collective-permute-start | bytes 1966088 | tf_op jit(solution)/shard_map/ppermute | solution.py:550
  34.0 38.1 %collective-permute-start.9 = (bf16[2,160,1024]{2,1,0:T(8,128)(2,1)S(1)}, bf16[2,160,1024]{2,1,0:T(8,128)(2,1)S(1)}, u32[]{:S(2)}, u32[]{:S(2)}) collective-permute-start(bf16[2,160,1024]{2,1,0:T(8,128)(2,1)S(1)} %get-tuple-element.33), channel_id=1, source_target_pairs={{0,4},{4,0},{8,12},{12,8},{16,20},{20,16},{24,28},{28,24},{1,5},{5... | collective-permute-start | bytes 1966088 | tf_op jit(solution)/shard_map/ppermute | solution.py:550
  34.5 15.7 %collective-permute-start.10 = (bf16[2,2,160,128]{3,2,1,0:T(8,128)(2,1)S(1)}, bf16[2,2,160,128]{3,2,1,0:T(8,128)(2,1)S(1)}, u32[]{:S(2)}, u32[]{:S(2)}) collective-permute-start(bf16[2,2,160,128]{3,2,1,0:T(8,128)(2,1)S(1)} %get-tuple-element.37), channel_id=1, source_target_pairs={{0,24},{4,28},{8,16},{12,20},{16,8},{20,12},{24,0},{28,4},{1,25},{... | collective-permute-start | bytes 491528 | tf_op jit(solution)/shard_map/ppermute | solution.py:550
  45.2 7.3 %collective-permute-start.11 = (bf16[2,2,160,128]{3,2,1,0:T(8,128)(2,1)S(1)}, bf16[2,2,160,128]{3,2,1,0:T(8,128)(2,1)S(1)}, u32[]{:S(2)}, u32[]{:S(2)}) collective-permute-start(bf16[2,2,160,128]{3,2,1,0:T(8,128)(2,1)S(1)} %get-tuple-element.38), channel_id=1, source_target_pairs={{0,8},{4,12},{8,0},{12,4},{16,24},{20,28},{24,16},{28,20},{1,9},{5... | collective-permute-start | bytes 491528 | tf_op jit(solution)/shard_map/ppermute | solution.py:550
  45.2 8.0 %collective-permute-start.12 = (bf16[2,2,160,128]{3,2,1,0:T(8,128)(2,1)S(1)}, bf16[2,2,160,128]{3,2,1,0:T(8,128)(2,1)S(1)}, u32[]{:S(2)}, u32[]{:S(2)}) collective-permute-start(bf16[2,2,160,128]{3,2,1,0:T(8,128)(2,1)S(1)} %get-tuple-element.39), channel_id=1, source_target_pairs={{0,16},{4,20},{8,24},{12,28},{16,0},{20,4},{24,8},{28,12},{1,17},{... | collective-permute-start | bytes 491528 | tf_op jit(solution)/shard_map/ppermute | solution.py:550
  53.3 18.1 %collective-permute-start.13 = (bf16[2,160,128]{2,1,0:T(8,128)(2,1)S(1)}, bf16[2,160,128]{2,1,0:T(8,128)(2,1)S(1)}, u32[]{:S(2)}, u32[]{:S(2)}) collective-permute-start(bf16[2,160,128]{2,1,0:T(8,128)(2,1)S(1)} %get-tuple-element.41), channel_id=1, source_target_pairs={{0,4},{4,0},{8,12},{12,8},{16,20},{20,16},{24,28},{28,24},{1,5},{5... | collective-permute-start | bytes 245768 | tf_op jit(solution)/shard_map/ppermute | solution.py:550
  53.3 4.5 %collective-permute-start.14 = (f32[2,256]{1,0:T(2,128)S(1)}, f32[2,256]{1,0:T(2,128)S(1)}, u32[]{:S(2)}, u32[]{:S(2)}) collective-permute-start(f32[2,256]{1,0:T(2,128)S(1)} %get-tuple-element.42.refs_4_), channel_id=1, source_target_pairs={{0,1},{1,0},{2,3},{3,2},{4,5},{5,4},{6,7},{7,6},{8,9},{9,8},{10,11... | collective-permute-start | bytes 6152 | tf_op jit(solution)/shard_map/ppermute | solution.py:555
  53.4 5.7 %collective-permute-start.15 = (f32[2,256]{1,0:T(2,128)S(1)}, f32[2,256]{1,0:T(2,128)S(1)}, u32[]{:S(2)}, u32[]{:S(2)}) collective-permute-start(f32[2,256]{1,0:T(2,128)S(1)} %get-tuple-element.42.refs_4_), channel_id=1, source_target_pairs={{0,2},{1,3},{2,0},{3,1},{4,6},{5,7},{6,4},{7,5},{8,10},{9,11},{10,... | collective-permute-start | bytes 6152 | tf_op jit(solution)/shard_map/ppermute | solution.py:555
  57.6 5.4 %collective-permute-start.16 = (f32[2,256]{1,0:T(2,128)S(1)}, f32[2,256]{1,0:T(2,128)S(1)}, u32[]{:S(2)}, u32[]{:S(2)}) collective-permute-start(f32[2,256]{1,0:T(2,128)S(1)} %get-tuple-element.42.refs_4_), channel_id=1, source_target_pairs={{0,3},{1,2},{2,1},{3,0},{4,7},{5,6},{6,5},{7,4},{8,11},{9,10},{10,... | collective-permute-start | bytes 6152 | tf_op jit(solution)/shard_map/ppermute | solution.py:555
  63.9 1.2 %collective-permute-start.18 = (f32[16,128]{1,0:T(8,128)S(1)}, f32[16,128]{1,0:T(8,128)S(1)}, u32[]{:S(2)}, u32[]{:S(2)}) collective-permute-start(f32[16,128]{1,0:T(8,128)S(1)} %router_part.1), channel_id=1, source_target_pairs={{0,4},{4,0},{8,12},{12,8},{16,20},{20,16},{24,28},{28,24},{1,5},{5... | collective-permute-start | bytes 24584 | tf_op jit(solution)/shard_map/ppermute | solution.py:550
  65.1 4.5 %collective-permute-start.19 = (f32[16,128]{1,0:T(8,128)S(1)}, f32[16,128]{1,0:T(8,128)S(1)}, u32[]{:S(2)}, u32[]{:S(2)}) collective-permute-start(f32[16,128]{1,0:T(8,128)S(1)} %add.8.refs_0_), channel_id=1, source_target_pairs={{0,24},{4,28},{8,16},{12,20},{16,8},{20,12},{24,0},{28,4},{1,25},{... | collective-permute-start | bytes 24584 | tf_op jit(solution)/shard_map/ppermute | solution.py:550
  67.7 3.7 %collective-permute-start.20 = (f32[16,128]{1,0:T(8,128)S(1)}, f32[16,128]{1,0:T(8,128)S(1)}, u32[]{:S(2)}, u32[]{:S(2)}) collective-permute-start(f32[16,128]{1,0:T(8,128)S(1)} %add.8.refs_0_), channel_id=1, source_target_pairs={{0,8},{4,12},{8,0},{12,4},{16,24},{20,28},{24,16},{28,20},{1,9},{5... | collective-permute-start | bytes 24584 | tf_op jit(solution)/shard_map/ppermute | solution.py:550
  67.7 3.7 %collective-permute-start.21 = (f32[16,128]{1,0:T(8,128)S(1)}, f32[16,128]{1,0:T(8,128)S(1)}, u32[]{:S(2)}, u32[]{:S(2)}) collective-permute-start(f32[16,128]{1,0:T(8,128)S(1)} %add.8.refs_0_), channel_id=1, source_target_pairs={{0,16},{4,20},{8,24},{12,28},{16,0},{20,4},{24,8},{28,12},{1,17},{... | collective-permute-start | bytes 24584 | tf_op jit(solution)/shard_map/ppermute | solution.py:550
